TPU v7x, 256 devices: a whole 4x4x8 slice. The times are simulated.
256 devices in a mesh: seq: 64 (over z, x, y_lo), sub: 4 (over y_hi, core).
Axes of the slice: x: 4, y: 4 (y_hi: 2, y_lo: 2; y = y_hi * 2 + y_lo), z: 8, core: 2. Of those that a mesh axis runs over, the one named last changes fastest.
Arguments:
- features: bfloat16 [262144, 768], P(('seq', 'sub')), may hold values from -6 to 6
- kernel: bfloat16 [3, 768, 384], replicated, may hold values from -0.125 to 0.125
- offsets: float32 [384], replicated, may hold values from -3 to 3
- mixer: bfloat16 [384, 768], replicated, may hold values from -0.3125 to 0.3125
- biases: float32 [768], replicated, may hold values from -3 to 3
- cotangent: bfloat16 [262144, 768], P(('seq', 'sub')), may hold values from -6 to 6
Outputs:
- layer_output: bfloat16 [262144, 768], P(('seq', 'sub'))
- input_grad: bfloat16 [262144, 768], P(('seq', 'sub'))
- kernel_grad: float32 [3, 768, 384], replicated
- offset_grad: float32 [384], replicated
- mixer_grad: float32 [384, 768], replicated
- biases_grad: float32 [768], replicated
All inputs are finite; a program needn't handle non-finite values.
Results may differ from a plain program's by a relative error of at most 0.0075.
Values may be sent and summed in bfloat16 or wider, within the bound.
A program may use at most 64 MiB of HBM per device.

v0:
```python
import math

import jax
import jax.numpy as jnp
from jax import lax
from jax.sharding import PartitionSpec as P

DILATION_STEP = 8192


def from_behind(value, axis, steps):
    count = lax.axis_size(axis)
    pairs = [(source, (source + steps) % count) for source in range(count)]
    return lax.ppermute(value, axis, pairs)


def gelu_exact(values):
    return jax.nn.gelu(values, approximate=False)


def gelu_slope(values):
    normal_cdf = 0.5 * (1.0 + jax.scipy.special.erf(values / math.sqrt(2.0)))
    return normal_cdf + values * jnp.exp(-0.5 * values * values) / math.sqrt(2.0 * math.pi)


def contract_rows(left, right):
    return lax.dot_general(
        left, right, (((0,), (0,)), ((), ())), preferred_element_type=jnp.float32
    )


def times_transposed(left, right):
    return lax.dot_general(
        left, right, (((1,), (1,)), ((), ())), preferred_element_type=jnp.float32
    )


def local(features, kernel, offsets, mixer, biases, cotangent):
    partition_rows = features.shape[0]
    offset_distance = DILATION_STEP // (partition_rows * lax.axis_size("sub"))
    factor = 1.0 / math.sqrt(partition_rows * lax.axis_size("seq") * lax.axis_size("sub"))
    inputs = features.astype(jnp.float32)
    activated_output = gelu_exact(inputs).astype(jnp.bfloat16)
    behind_neighbor = from_behind(activated_output, "seq", offset_distance)
    ahead_neighbor = from_behind(activated_output, "seq", -offset_distance)
    tap_early = jnp.dot(behind_neighbor, kernel[0], preferred_element_type=jnp.float32).astype(
        jnp.bfloat16
    )
    tap_late = jnp.dot(ahead_neighbor, kernel[2], preferred_element_type=jnp.float32).astype(
        jnp.bfloat16
    )
    preact = (
        jnp.dot(activated_output, kernel[1], preferred_element_type=jnp.float32)
        + tap_early.astype(jnp.float32)
        + tap_late.astype(jnp.float32)
        + offsets
    )
    hidden = gelu_exact(preact).astype(jnp.bfloat16)
    layer_output = (
        inputs + jnp.dot(hidden, mixer, preferred_element_type=jnp.float32) + biases
    ).astype(jnp.bfloat16)
    cot_float = cotangent.astype(jnp.float32)
    mixer_part = contract_rows(hidden, cotangent) * factor
    biases_part = jnp.sum(cot_float, axis=0) * factor
    hidden_grad = times_transposed(cotangent, mixer)
    preactivation_grad = (hidden_grad * gelu_slope(preact)).astype(jnp.bfloat16)
    grad_later = from_behind(preactivation_grad, "seq", -offset_distance)
    grad_earlier = from_behind(preactivation_grad, "seq", offset_distance)
    kernel_part = (
        jnp.stack(
            [
                contract_rows(behind_neighbor, preactivation_grad),
                contract_rows(activated_output, preactivation_grad),
                contract_rows(ahead_neighbor, preactivation_grad),
            ]
        )
        * factor
    )
    offset_part = jnp.sum(preactivation_grad.astype(jnp.float32), axis=0) * factor
    activated_output_grad = (
        times_transposed(preactivation_grad, kernel[1])
        + times_transposed(grad_later, kernel[0])
        + times_transposed(grad_earlier, kernel[2])
    )
    input_grad = (cot_float + activated_output_grad * gelu_slope(inputs)).astype(jnp.bfloat16)
    kernel_grad, offset_grad, mixer_grad, biases_grad = lax.psum(
        (kernel_part, offset_part, mixer_part, biases_part), ("seq", "sub")
    )
    return (layer_output, input_grad, kernel_grad, offset_grad, mixer_grad, biases_grad)


def solution(mesh):
    placed = (P(("seq", "sub"), None), P(), P(), P(), P(), P(("seq", "sub"), None))
    return jax.shard_map(
        local,
        mesh=mesh,
        in_specs=placed,
        out_specs=(P(("seq", "sub"), None), P(("seq", "sub"), None), P(), P(), P(), P()),
        check_vma=False,
    )
```

profile of v0, /device:TPU:1, one launch (start us, length us, event | category | flops | bytes accessed | tf_op | source)
XLA Modules:
  0.0 361.3 jit_solution(16244825312015924601)
XLA Ops:
  7.2 0.0 copy-start
  7.2 0.0 all-reduce.4.cloned.1.call-start
  7.2 0.0 copy-start.5
  7.2 8.0 %fusion.3 = bf16[1024,768]{1,0:T(8,128)(2,1)S(1)} fusion(bf16[1024,768]{1,0:T(8,128)(2,1)} %param.6), kind=kLoop, calls=%fused_computation.14 | loop fusion | flops 51904512 | bytes 3145728 | tf_op jit(solution)/shard_map/convert_element_type | solution.py:43
  15.3 2.1 collective-permute-start
  17.4 6.8 %collective-permute-start.1 = (bf16[1024,768]{1,0:T(8,128)(2,1)S(1)}, bf16[1024,768]{1,0:T(8,128)(2,1)S(1)}, u32[]{:S(2)}, u32[]{:S(2)}) collective-permute-start(bf16[1024,768]{1,0:T(8,128)(2,1)S(1)} %fusion.3), channel_id=1, source_target_pairs={{0,248},{4,252},{8,0},{12,4},{16,8},{20,12},{24,16},{28,20},{32,24... | collective-permute-start | bytes 4718600 | tf_op jit(solution)/shard_map/ppermute | solution.py:14
  24.2 0.0 copy-done.5
  24.2 1.0 fusion.64
  25.2 0.0 copy-start.8
  25.2 32.9 %collective-permute-done = bf16[1024,768]{1,0:T(8,128)(2,1)S(1)} collective-permute-done((bf16[1024,768]{1,0:T(8,128)(2,1)S(1)}, bf16[1024,768]{1,0:T(8,128)(2,1)S(1)}, u32[]{:S(2)}, u32[]{:S(2)}) %collective-permute-start) | collective-permute-done | bytes 1572896 | tf_op jit(solution)/shard_map/ppermute | solution.py:14
  58.1 1.0 convolution_convert_fusion.1
  59.1 0.0 copy-start.1
  59.1 0.0 collective-permute-done.1
  59.1 0.0 copy-done.8
  59.1 4.3 %fusion.43 = (bf16[1024,384]{1,0:T(8,128)(2,1)S(1)}, f32[1024,384]{1,0:T(8,128)S(1)}) fusion(f32[384]{0:T(512)S(1)} %copy-done.8, bf16[1024,768]{1,0:T(8,128)(2,1)S(1)} %collective-permute-done.1, bf16[3,768,384]{2,1,0:T(8,128)(2,1)S(1)} %copy-done.5, f32[1024,384]{1,0:T(8,128)S(1)} %fusion.64, bf16[1024,384]{1,0:T(8,128)(2,1)S(1)} %convolution_convert_fusion.1), kind=kOutput, calls=%fused_computation.56 | convolution fusion | flops 631898112 | bytes 6883328 | tf_op jit(solution)/shard_map/dot_general | solution.py:49
  63.4 0.0 copy-done
  63.4 0.0 copy-done.1
  63.4 2.2 convert_reduce_fusion.1
  65.6 2.1 convolution_bitcast_fusion.1
  67.8 1.8 convolution_multiply_fusion
  69.6 2.1 convolution_bitcast_fusion
  71.7 2.1 convolution_bitcast_fusion.2
  73.9 2.0 maximum_multiply_fusion
  75.9 0.0 all-reduce.4.cloned.1.call-update
  75.9 0.3 convert_reduce_fusion
  76.2 0.0 copy-start.7
  76.2 3.8 %collective-permute-start.2 = (bf16[1024,384]{1,0:T(8,128)(2,1)}, bf16[1024,384]{1,0:T(8,128)(2,1)}, u32[]{:S(2)}, u32[]{:S(2)}) collective-permute-start(bf16[1024,384]{1,0:T(8,128)(2,1)} %get-tuple-element.13), channel_id=1, source_target_pairs={{0,248},{4,252},{8,0},{12,4},{16,8},{20,12},{24,16},{28,20},{32,24... | collective-permute-start | bytes 2359304 | tf_op jit(solution)/shard_map/ppermute | solution.py:14
  80.0 0.0 collective-permute-start.3
  80.0 4.0 %fusion.62 = f32[1024,768]{1,0:T(8,128)} fusion(bf16[1024,384]{1,0:T(8,128)(2,1)} %get-tuple-element.13, bf16[3,768,384]{2,1,0:T(8,128)(2,1)} %param.7), kind=kOutput, calls=%fused_computation.91 | convolution fusion | flops 603979776 | bytes 4521984 | tf_op jit(solution)/shard_map/dot_general | solution.py:33
  84.0 83.8 %all-reduce = (f32[384]{0:T(512)}, f32[768]{0:T(1024)}) all-reduce(f32[384]{0:T(512)S(1)} %broadcast_multiply_fusion.1, f32[768]{0:T(1024)S(1)} %broadcast_multiply_fusion), channel_id=1, replica_groups=mesh['seq'=64,'sub'=4] {'seq','sub'}, use_global_device_ids=true, to_apply=%region_2.0 | all-reduce | flops 1152 | bytes 9216 | tf_op jit(solution)/shard_map/psum | solution.py:86
  167.8 0.0 copy-done.7
  167.8 0.0 copy-start.6
  167.8 0.0 copy-start.3
  167.8 3.7 %fusion.33 = bf16[1024,768]{1,0:T(8,128)(2,1)} fusion(bf16[1024,768]{1,0:T(8,128)(2,1)} %param.6, bf16[1024,384]{1,0:T(8,128)(2,1)S(1)} %get-tuple-element.10, bf16[384,768]{1,0:T(8,128)(2,1)S(1)} %copy-done, f32[768]{0:T(1024)S(1)} %copy-done.7), kind=kOutput, calls=%fused_computation.44 | convolution fusion | flops 607125504 | bytes 4525056 | tf_op jit(solution)/shard_map/dot_general | solution.py:60
  171.5 0.0 copy-start.2
  171.5 0.0 collective-permute-done.2
  171.5 0.0 copy-done.6
  171.5 2.3 fusion.59
  173.8 0.0 collective-permute-done.3
  173.8 0.0 copy-done.3
  173.8 0.0 copy-done.2
  173.9 4.6 %fusion = bf16[1024,768]{1,0:T(8,128)(2,1)} fusion(bf16[1024,768]{1,0:T(8,128)(2,1)S(1)} %copy-done.1, bf16[1024,768]{1,0:T(8,128)(2,1)S(1)} %copy-done.3, f32[1024,768]{1,0:T(8,128)S(1)} %copy-done.2, f32[1024,768]{1,0:T(8,128)S(1)} %fusion.59, bf16[1024,384]{1,0:T(8,128)(2,1)} %collective-permute-done.3, bf16[3,768,384]{2,1,0:T(8,128)(2,1)S(1)} %copy-done.6), kind=kOutput, calls=%fused_computation.11 | convolution fusion | flops 615776256 | bytes 12386304 | tf_op jit(solution)/shard_map/dot_general | solution.py:33
  178.4 170.8 %all-reduce.4.cloned.1.call-done = (f32[3,768,384]{2,1,0:T(8,128)}, f32[384,768]{1,0:T(8,128)}) async-done(((f32[3,768,384]{2,1,0:T(8,128)}, f32[384,768]{1,0:T(8,128)}), (f32[3,768,384]{2,1,0:T(8,128)}, f32[384,768]{1,0:T(8,128)})) %all-reduce.4.cloned.1.call-update) | async-done | bytes 4718608 | tf_op jit(solution)/shard_map/psum | solution.py:86
  349.3 0.0 copy-start.4
  349.3 4.1 %copy.14 = f32[3,768,384]{2,1,0:T(8,128)} copy(f32[3,768,384]{2,1,0:T(8,128)} %get-tuple-element.16) | data formatting | bytes 7077888
  353.4 0.0 copy-done.4
  353.4 1.0 copy.15
  (2 shorter events, 0.0 us)
Async XLA Ops:
  7.2 56.2 %copy-start = (bf16[384,768]{1,0:T(8,128)(2,1)S(1)}, bf16[384,768]{1,0:T(8,128)(2,1)}, u32[]{:S(2)}) copy-start(bf16[384,768]{1,0:T(8,128)(2,1)} %param.9) | copy-start | bytes 1769476
  7.2 342.1 %all-reduce.4.cloned.1.call-start = ((), (), s32[]{:S(2)}) async-start(), calls=%async_computation | async-start | bytes 9437184 | tf_op jit(solution)/shard_map/psum | solution.py:86
  7.2 17.0 %copy-start.5 = (bf16[3,768,384]{2,1,0:T(8,128)(2,1)S(1)}, bf16[3,768,384]{2,1,0:T(8,128)(2,1)}, u32[]{:S(2)}) copy-start(bf16[3,768,384]{2,1,0:T(8,128)(2,1)} %param.7) | copy-start | bytes 5308420
  15.3 42.8 %collective-permute-start = (bf16[1024,768]{1,0:T(8,128)(2,1)S(1)}, bf16[1024,768]{1,0:T(8,128)(2,1)S(1)}, u32[]{:S(2)}, u32[]{:S(2)}) collective-permute-start(bf16[1024,768]{1,0:T(8,128)(2,1)S(1)} %fusion.3), channel_id=1, source_target_pairs={{0,8},{4,12},{8,16},{12,20},{16,24},{20,28},{24,32},{28,36},{32,40... | collective-permute-start | bytes 4718600 | tf_op jit(solution)/shard_map/ppermute | solution.py:14
  17.4 41.7 %collective-permute-start.1 = (bf16[1024,768]{1,0:T(8,128)(2,1)S(1)}, bf16[1024,768]{1,0:T(8,128)(2,1)S(1)}, u32[]{:S(2)}, u32[]{:S(2)}) collective-permute-start(bf16[1024,768]{1,0:T(8,128)(2,1)S(1)} %fusion.3), channel_id=1, source_target_pairs={{0,248},{4,252},{8,0},{12,4},{16,8},{20,12},{24,16},{28,20},{32,24... | collective-permute-start | bytes 4718600 | tf_op jit(solution)/shard_map/ppermute | solution.py:14
  25.2 33.9 %copy-start.8 = (f32[384]{0:T(512)S(1)}, f32[384]{0:T(512)}, u32[]{:S(2)}) copy-start(f32[384]{0:T(512)} %param.8) | copy-start | bytes 4612
  59.1 4.3 %copy-start.1 = (bf16[1024,768]{1,0:T(8,128)(2,1)S(1)}, bf16[1024,768]{1,0:T(8,128)(2,1)}, u32[]{:S(2)}) copy-start(bf16[1024,768]{1,0:T(8,128)(2,1)} %param.11) | copy-start | bytes 4718596
  76.2 91.6 %copy-start.7 = (f32[768]{0:T(1024)S(1)}, f32[768]{0:T(1024)}, u32[]{:S(2)}) copy-start(f32[768]{0:T(1024)} %param.10) | copy-start | bytes 9220
  76.2 95.3 %collective-permute-start.2 = (bf16[1024,384]{1,0:T(8,128)(2,1)}, bf16[1024,384]{1,0:T(8,128)(2,1)}, u32[]{:S(2)}, u32[]{:S(2)}) collective-permute-start(bf16[1024,384]{1,0:T(8,128)(2,1)} %get-tuple-element.13), channel_id=1, source_target_pairs={{0,248},{4,252},{8,0},{12,4},{16,8},{20,12},{24,16},{28,20},{32,24... | collective-permute-start | bytes 2359304 | tf_op jit(solution)/shard_map/ppermute | solution.py:14
  80.0 93.8 %collective-permute-start.3 = (bf16[1024,384]{1,0:T(8,128)(2,1)}, bf16[1024,384]{1,0:T(8,128)(2,1)}, u32[]{:S(2)}, u32[]{:S(2)}) collective-permute-start(bf16[1024,384]{1,0:T(8,128)(2,1)} %get-tuple-element.13), channel_id=1, source_target_pairs={{0,8},{4,12},{8,16},{12,20},{16,24},{20,28},{24,32},{28,36},{32,40... | collective-permute-start | bytes 2359304 | tf_op jit(solution)/shard_map/ppermute | solution.py:14
  167.8 3.7 %copy-start.6 = (bf16[3,768,384]{2,1,0:T(8,128)(2,1)S(1)}, bf16[3,768,384]{2,1,0:T(8,128)(2,1)}, u32[]{:S(2)}) copy-start(bf16[3,768,384]{2,1,0:T(8,128)(2,1)} %param.7) | copy-start | bytes 5308420
  167.8 6.0 %copy-start.3 = (bf16[1024,768]{1,0:T(8,128)(2,1)S(1)}, bf16[1024,768]{1,0:T(8,128)(2,1)}, u32[]{:S(2)}) copy-start(bf16[1024,768]{1,0:T(8,128)(2,1)} %param.6) | copy-start | bytes 4718596
  171.5 2.3 copy-start.2
  349.3 4.1 %copy-start.4 = (f32[384,768]{1,0:T(8,128)S(1)}, f32[384,768]{1,0:T(8,128)}, u32[]{:S(2)}) copy-start(f32[384,768]{1,0:T(8,128)} %get-tuple-element.18) | copy-start | bytes 3538948
Sparse Core Ops, SparseCore 0:
  76.0 273.2 all-reduce.3
where the time goes:
time: 362 us; the launch traced here: 361 us
  waiting for transfers between devices  204 us (56%)
  blocking collectives  83.8 us (23%)
  matrix products  31.2 us (9%)
  between operations  14.2 us (4%)
  starting transfers between devices  12.8 us (4%)
  other arithmetic  10.4 us (3%)
  local copies, waits for them, and re-layouts  5.18 us (1%)
    psum x1, waiting for transfers between devices, local(): lax.psum((kernel_part, offset_part, mixer_part, biases_part), ('seq', 'su...  171 us
    psum x1, blocking collectives, local(): lax.psum((kernel_part, offset_part, mixer_part, biases_part), ('seq', 'su...  83.8 us
    ppermute x4, waiting for transfers between devices, from_behind(): return lax.ppermute(value, axis, pairs)  32.9 us
    dot_general x4, matrix products, times_transposed(): lax.dot_general(left, right, (((1,), (1,)), ((), ())), preferred_element_...  13.1 us
    ppermute x4, starting transfers between devices, from_behind(): return lax.ppermute(value, axis, pairs)  12.7 us
    dot_general x4, matrix products, contract_rows(): lax.dot_general(left, right, (((0,), (0,)), ((), ())), preferred_element_...  8.25 us
    convert_element_type x1, other arithmetic, local(): activated_output = gelu_exact(inputs).astype(jnp.bfloat16)  8.04 us
  transfers between devices with their start and end apart: 5, of which 2 were waited for; matrix products, arithmetic and copies ran while one was open for 5% of the time, Pallas kernels for 0%

commit v1 on v0

--- a/solution.py
+++ b/solution.py
@@ -41,14 +41,14 @@
     factor = 1.0 / math.sqrt(partition_rows * lax.axis_size("seq") * lax.axis_size("sub"))
     inputs = features.astype(jnp.float32)
     activated_output = gelu_exact(inputs).astype(jnp.bfloat16)
-    behind_neighbor = from_behind(activated_output, "seq", offset_distance)
-    ahead_neighbor = from_behind(activated_output, "seq", -offset_distance)
-    tap_early = jnp.dot(behind_neighbor, kernel[0], preferred_element_type=jnp.float32).astype(
+    send_early = jnp.dot(activated_output, kernel[0], preferred_element_type=jnp.float32).astype(
         jnp.bfloat16
     )
-    tap_late = jnp.dot(ahead_neighbor, kernel[2], preferred_element_type=jnp.float32).astype(
+    send_late = jnp.dot(activated_output, kernel[2], preferred_element_type=jnp.float32).astype(
         jnp.bfloat16
     )
+    tap_early = from_behind(send_early, "seq", offset_distance)
+    tap_late = from_behind(send_late, "seq", -offset_distance)
     preact = (
         jnp.dot(activated_output, kernel[1], preferred_element_type=jnp.float32)
         + tap_early.astype(jnp.float32)
@@ -69,9 +69,9 @@
     kernel_part = (
         jnp.stack(
             [
-                contract_rows(behind_neighbor, preactivation_grad),
+                contract_rows(activated_output, grad_later),
                 contract_rows(activated_output, preactivation_grad),
-                contract_rows(ahead_neighbor, preactivation_grad),
+                contract_rows(activated_output, grad_earlier),
             ]
         )
         * factor

time: 362 us -> 359 us (level)
  matrix products: 31.2 us -> 21.4 us
  waiting for transfers between devices: 204 us -> 213 us
  blocking collectives: 83.8 us -> 77.3 us
    psum x1, waiting for transfers between devices: 171 us -> 184 us  [local(): lax.psum((kernel_part, offset_part, mixer_part, biases_part), ('seq', 'su...]
    psum x1, blocking collectives: 83.8 us -> 77.3 us  [local(): lax.psum((kernel_part, offset_part, mixer_part, biases_part), ('seq', 'su...]
    dot_general x4, matrix products: 13.1 us -> 8.21 us  [times_transposed(): lax.dot_general(left, right, (((1,), (1,)), ((), ())), preferred_element_...]
  transfers between devices with their start and end apart: 5 -> 5, of which waited for: 2 -> 3; matrix products, arithmetic and copies ran while one was open for 5% -> 4% of each run, Pallas kernels for 0% -> 0%
where the time goes in v1:
time: 359 us; the launch traced here: 358 us
  waiting for transfers between devices  213 us (59%)
  blocking collectives  77.3 us (22%)
  matrix products  21.4 us (6%)
  starting transfers between devices  14.7 us (4%)
  between operations  14.2 us (4%)
  other arithmetic  10.4 us (3%)
  local copies, waits for them, and re-layouts  6.19 us (2%)
    psum x1, waiting for transfers between devices, local(): lax.psum((kernel_part, offset_part, mixer_part, biases_part), ('seq', 'su...  184 us
    psum x1, blocking collectives, local(): lax.psum((kernel_part, offset_part, mixer_part, biases_part), ('seq', 'su...  77.3 us
    ppermute x4, waiting for transfers between devices, from_behind(): return lax.ppermute(value, axis, pairs)  29.4 us
    ppermute x4, starting transfers between devices, from_behind(): return lax.ppermute(value, axis, pairs)  14.6 us
    dot_general x4, matrix products, times_transposed(): lax.dot_general(left, right, (((1,), (1,)), ((), ())), preferred_element_...  8.21 us
    convert_element_type x1, other arithmetic, local(): activated_output = gelu_exact(inputs).astype(jnp.bfloat16)  8.04 us
  transfers between devices with their start and end apart: 5, of which 3 were waited for; matrix products, arithmetic and copies ran while one was open for 4% of the time, Pallas kernels for 0%

profile of v1, /device:TPU:1, one launch (start us, length us, event | category | flops | bytes accessed | tf_op | source)
XLA Modules:
  0.0 357.6 jit_solution(11011791587891050671)
XLA Ops:
  7.2 0.0 copy-start
  7.2 0.0 all-reduce.4.cloned.1.call-start
  7.2 0.0 copy-start.4
  7.2 8.0 %fusion.3 = bf16[1024,768]{1,0:T(8,128)(2,1)S(1)} fusion(bf16[1024,768]{1,0:T(8,128)(2,1)} %param.6), kind=kLoop, calls=%fused_computation.14 | loop fusion | flops 51904512 | bytes 3145728 | tf_op jit(solution)/shard_map/convert_element_type | solution.py:43
  15.3 0.0 copy-done.4
  15.3 1.0 convolution_convert_fusion.1
  16.3 0.0 copy-start.12
  16.3 2.1 collective-permute-start
  18.4 1.0 convolution_convert_fusion
  19.4 0.0 copy-start.1
  19.4 6.6 %collective-permute-start.1 = (bf16[1024,384]{1,0:T(8,128)(2,1)S(1)}, bf16[1024,384]{1,0:T(8,128)(2,1)S(1)}, u32[]{:S(2)}, u32[]{:S(2)}) collective-permute-start(bf16[1024,384]{1,0:T(8,128)(2,1)S(1)} %convolution_convert_fusion), channel_id=1, source_target_pairs={{0,248},{4,252},{8,0},{12,4},{16,8},{20,12},{24,16},{28,20},{32,24... | collective-permute-start | bytes 2359304 | tf_op jit(solution)/shard_map/ppermute | solution.py:14
  26.0 16.2 %collective-permute-done = bf16[1024,384]{1,0:T(8,128)(2,1)S(1)} collective-permute-done((bf16[1024,384]{1,0:T(8,128)(2,1)S(1)}, bf16[1024,384]{1,0:T(8,128)(2,1)S(1)}, u32[]{:S(2)}, u32[]{:S(2)}) %collective-permute-start) | collective-permute-done | bytes 786464 | tf_op jit(solution)/shard_map/ppermute | solution.py:14
  42.2 0.0 collective-permute-done.1
  42.3 0.0 copy-done.12
  42.3 4.3 %fusion.43 = (bf16[1024,384]{1,0:T(8,128)(2,1)S(1)}, f32[1024,384]{1,0:T(8,128)S(1)}) fusion(f32[384]{0:T(512)S(1)} %copy-done.12, bf16[1024,384]{1,0:T(8,128)(2,1)S(1)} %collective-permute-done.1, bf16[1024,384]{1,0:T(8,128)(2,1)S(1)} %collective-permute-done, bf16[1024,768]{1,0:T(8,128)(2,1)S(1)} %fusion.3, bf16[3,768,384]{2,1,0:T(8,128)(2,1)S(1)} %copy-done.4), kind=kOutput, calls=%fused_computation.56 | convolution fusion | flops 631504896 | bytes 6096896 | tf_op jit(solution)/shard_map/dot_general | solution.py:53
  46.6 0.0 copy-done
  46.6 0.0 copy-done.1
  46.6 1.3 convert_reduce_fusion.1
  47.9 0.0 copy-start.6
  48.0 0.1 collective-permute-start.3
  48.0 5.8 %collective-permute-start.2 = (bf16[1024,384]{1,0:T(8,128)(2,1)S(1)}, bf16[1024,384]{1,0:T(8,128)(2,1)S(1)}, u32[]{:S(2)}, u32[]{:S(2)}) collective-permute-start(bf16[1024,384]{1,0:T(8,128)(2,1)S(1)} %get-tuple-element.13), channel_id=1, source_target_pairs={{0,248},{4,252},{8,0},{12,4},{16,8},{20,12},{24,16},{28,20},{32,24... | collective-permute-start | bytes 2359304 | tf_op jit(solution)/shard_map/ppermute | solution.py:14
  53.8 1.0 convolution_bitcast_fusion.1
  54.8 0.0 copy-done.6
  54.8 1.8 convolution_multiply_fusion
  56.7 13.2 %collective-permute-done.3 = bf16[1024,384]{1,0:T(8,128)(2,1)S(1)} collective-permute-done((bf16[1024,384]{1,0:T(8,128)(2,1)S(1)}, bf16[1024,384]{1,0:T(8,128)(2,1)S(1)}, u32[]{:S(2)}, u32[]{:S(2)}) %collective-permute-start.3) | collective-permute-done | bytes 786464 | tf_op jit(solution)/shard_map/ppermute | solution.py:14
  69.9 0.0 copy-start.9
  69.9 1.0 convolution_bitcast_fusion
  70.9 0.0 copy-done.9
  70.9 0.0 collective-permute-done.2
  70.9 0.0 copy-start.7
  70.9 0.9 copy-done.7
  71.8 1.0 convolution_bitcast_fusion.2
  72.8 2.0 maximum_multiply_fusion
  74.8 0.0 all-reduce.4.cloned.1.call-update
  74.8 0.3 convert_reduce_fusion
  75.1 77.3 %all-reduce = (f32[384]{0:T(512)}, f32[768]{0:T(1024)}) all-reduce(f32[384]{0:T(512)S(1)} %broadcast_multiply_fusion.1, f32[768]{0:T(1024)S(1)} %broadcast_multiply_fusion), channel_id=1, replica_groups=mesh['seq'=64,'sub'=4] {'seq','sub'}, use_global_device_ids=true, to_apply=%region_2.0 | all-reduce | flops 1152 | bytes 9216 | tf_op jit(solution)/shard_map/psum | solution.py:86
  152.4 0.0 copy-start.2
  152.4 0.0 copy-start.11
  152.4 2.4 fusion.62
  154.9 0.0 copy-done.2
  154.9 0.0 copy-done.11
  154.9 0.0 copy-start.5
  154.9 0.0 copy-start.8
  154.9 2.1 fusion.33
  157.0 0.0 copy-done.5
  157.0 0.0 copy-done.8
  157.0 0.0 copy-start.10
  157.0 1.0 fusion.59
  158.0 0.1 copy-done.10
  158.2 3.4 fusion
  161.6 184.0 %all-reduce.4.cloned.1.call-done = (f32[3,768,384]{2,1,0:T(8,128)}, f32[384,768]{1,0:T(8,128)}) async-done(((f32[3,768,384]{2,1,0:T(8,128)}, f32[384,768]{1,0:T(8,128)}), (f32[3,768,384]{2,1,0:T(8,128)}, f32[384,768]{1,0:T(8,128)})) %all-reduce.4.cloned.1.call-update) | async-done | bytes 4718608 | tf_op jit(solution)/shard_map/psum | solution.py:86
  345.6 0.0 copy-start.3
  345.6 4.1 %copy.14 = f32[3,768,384]{2,1,0:T(8,128)} copy(f32[3,768,384]{2,1,0:T(8,128)} %get-tuple-element.16) | data formatting | bytes 7077888
  349.8 0.0 copy-done.3
  349.8 1.0 copy.15
  (2 shorter events, 0.0 us)
Async XLA Ops:
  7.2 39.4 %copy-start = (bf16[384,768]{1,0:T(8,128)(2,1)S(1)}, bf16[384,768]{1,0:T(8,128)(2,1)}, u32[]{:S(2)}) copy-start(bf16[384,768]{1,0:T(8,128)(2,1)} %param.9) | copy-start | bytes 1769476
  7.2 338.5 %all-reduce.4.cloned.1.call-start = ((), (), s32[]{:S(2)}) async-start(), calls=%async_computation | async-start | bytes 9437184 | tf_op jit(solution)/shard_map/psum | solution.py:86
  7.2 8.1 %copy-start.4 = (bf16[3,768,384]{2,1,0:T(8,128)(2,1)S(1)}, bf16[3,768,384]{2,1,0:T(8,128)(2,1)}, u32[]{:S(2)}) copy-start(bf16[3,768,384]{2,1,0:T(8,128)(2,1)} %param.7) | copy-start | bytes 5308420
  16.3 26.0 %copy-start.12 = (f32[384]{0:T(512)S(1)}, f32[384]{0:T(512)}, u32[]{:S(2)}) copy-start(f32[384]{0:T(512)} %param.8) | copy-start | bytes 4612
  16.3 25.9 %collective-permute-start = (bf16[1024,384]{1,0:T(8,128)(2,1)S(1)}, bf16[1024,384]{1,0:T(8,128)(2,1)S(1)}, u32[]{:S(2)}, u32[]{:S(2)}) collective-permute-start(bf16[1024,384]{1,0:T(8,128)(2,1)S(1)} %convolution_convert_fusion.1), channel_id=1, source_target_pairs={{0,8},{4,12},{8,16},{12,20},{16,24},{20,28},{24,32},{28,36},{32,40... | collective-permute-start | bytes 2359304 | tf_op jit(solution)/shard_map/ppermute | solution.py:14
  19.4 27.2 %copy-start.1 = (bf16[1024,768]{1,0:T(8,128)(2,1)S(1)}, bf16[1024,768]{1,0:T(8,128)(2,1)}, u32[]{:S(2)}) copy-start(bf16[1024,768]{1,0:T(8,128)(2,1)} %param.11) | copy-start | bytes 4718596
  19.4 22.9 %collective-permute-start.1 = (bf16[1024,384]{1,0:T(8,128)(2,1)S(1)}, bf16[1024,384]{1,0:T(8,128)(2,1)S(1)}, u32[]{:S(2)}, u32[]{:S(2)}) collective-permute-start(bf16[1024,384]{1,0:T(8,128)(2,1)S(1)} %convolution_convert_fusion), channel_id=1, source_target_pairs={{0,248},{4,252},{8,0},{12,4},{16,8},{20,12},{24,16},{28,20},{32,24... | collective-permute-start | bytes 2359304 | tf_op jit(solution)/shard_map/ppermute | solution.py:14
  47.9 6.9 %copy-start.6 = (bf16[1024,384]{1,0:T(8,128)(2,1)}, bf16[1024,384]{1,0:T(8,128)(2,1)S(1)}, u32[]{:S(2)}) copy-start(bf16[1024,384]{1,0:T(8,128)(2,1)S(1)} %get-tuple-element.13) | copy-start | bytes 2359300
  48.0 21.9 %collective-permute-start.3 = (bf16[1024,384]{1,0:T(8,128)(2,1)S(1)}, bf16[1024,384]{1,0:T(8,128)(2,1)S(1)}, u32[]{:S(2)}, u32[]{:S(2)}) collective-permute-start(bf16[1024,384]{1,0:T(8,128)(2,1)S(1)} %get-tuple-element.13), channel_id=1, source_target_pairs={{0,8},{4,12},{8,16},{12,20},{16,24},{20,28},{24,32},{28,36},{32,40... | collective-permute-start | bytes 2359304 | tf_op jit(solution)/shard_map/ppermute | solution.py:14
  48.0 22.8 %collective-permute-start.2 = (bf16[1024,384]{1,0:T(8,128)(2,1)S(1)}, bf16[1024,384]{1,0:T(8,128)(2,1)S(1)}, u32[]{:S(2)}, u32[]{:S(2)}) collective-permute-start(bf16[1024,384]{1,0:T(8,128)(2,1)S(1)} %get-tuple-element.13), channel_id=1, source_target_pairs={{0,248},{4,252},{8,0},{12,4},{16,8},{20,12},{24,16},{28,20},{32,24... | collective-permute-start | bytes 2359304 | tf_op jit(solution)/shard_map/ppermute | solution.py:14
  69.9 1.0 copy-start.9
  70.9 0.9 copy-start.7
  152.4 2.4 copy-start.2
  152.4 2.4 copy-start.11
  154.9 2.1 copy-start.5
  154.9 2.1 copy-start.8
  157.0 1.1 copy-start.10
  345.6 4.1 %copy-start.3 = (f32[384,768]{1,0:T(8,128)S(1)}, f32[384,768]{1,0:T(8,128)}, u32[]{:S(2)}) copy-start(f32[384,768]{1,0:T(8,128)} %get-tuple-element.18) | copy-start | bytes 3538948
Sparse Core Ops, SparseCore 0:
  75.0 270.6 all-reduce.3

commit v2 on v1

v2 whole, which is shorter than its diff:
```python
import math

import jax
import jax.numpy as jnp
from jax import lax
from jax.experimental import pallas as pl
from jax.experimental.pallas import tpu as pltpu
from jax.sharding import PartitionSpec as P

MESH = pl.DeviceIdType.MESH
BF = jnp.bfloat16
F32 = jnp.float32

DILATION_STEP = 8192
C = 768
H = 384
ROWS = 1024
W = 128
NC = H // W
NR = 4
RB = ROWS // NR

NX, NY, NZ = 4, 4, 8

KG1_AT = 0
MG_AT = NC * C
KG02_AT = MG_AT + (H // W) * (C // W) * W
TOTAL = KG02_AT + 2 * NC * C
SEGS = ((0, 4096), (4096, 2048), (6144, 1024), (7168, 2048))
VEC = 16

T_SCALE = 0.3
TAIL = (
    0.11962923731872051,
    0.12075488221323095,
    0.0999078411835699,
    0.12857978094297895,
    -0.05371691656802647,
    0.20638841535029362,
    -0.1572225638776185,
    0.03567924927328374,
)


def gelu_and_slope(v):
    u = jnp.abs(v)
    t = 1.0 / (1.0 + T_SCALE * u)
    poly = TAIL[-1]
    for coef in TAIL[-2::-1]:
        poly = poly * t + coef
    bell = jnp.exp(-0.5 * u * u)
    tail = poly * t * bell
    cdf = jnp.where(v >= 0.0, 1.0 - tail, tail)
    return v * cdf, cdf + v * bell * (1.0 / math.sqrt(2.0 * math.pi))


def nn(a, b):
    return jnp.dot(a, b, preferred_element_type=F32)


def nt(a, b):
    return lax.dot_general(a, b, (((1,), (1,)), ((), ())), preferred_element_type=F32)


def position():
    seq, sub = lax.axis_index("seq"), lax.axis_index("sub")
    z, x = lax.div(seq, 2 * NX), lax.rem(lax.div(seq, 2), NX)
    y = lax.div(sub, 2) * 2 + lax.rem(seq, 2)
    return seq, sub, x, y, z, lax.rem(sub, 2)


def device(x, y, z, core):
    return (z * (2 * NX) + x * 2 + lax.rem(y, 2), lax.div(y, 2) * 2 + core)


def main_kernel(
    f_hbm, k_hbm, off_ref, mix_hbm, bias_ref, cot_hbm,
    lo_hbm, ig_hbm, gg_hbm, vec_ref,
    f_v, cot_v, kw_v, k1_v, mix_v,
    act_v, actt_v, slope_v, pre_v, hg_v,
    t0_v, t2_v, te_v, tl_v, hid_v, hidt_v, pg_v, pg02_v,
    lo_v, ig_v, g_v, sbc, rbc, sby, rby, sbz, rbz, sbx, rbx, gg_v,
    vs, vc, vy, vz, vx,
    f_sem, in_sem, out_sem, halo_send, tap_recv, pg_recv, seg_send, seg_recv, vec_send, vec_recv,
):
    seq, sub, x, y, z, core = position()
    nseq = 2 * NX * NZ
    ahead = (lax.rem(seq + 2, nseq), sub)
    behind = (lax.rem(seq + nseq - 2, nseq), sub)

    def y_peer(d):
        return device(x, lax.rem(y + d, NY), z, core)

    def z_peer(d):
        return device(x, y, lax.rem(z + d, NZ), core)

    def x_peer(d):
        return device(lax.rem(x + d, NX), y, z, core)

    sibling = device(x, y, z, 1 - core)

    barrier = pltpu.get_barrier_semaphore()

    def greet(to):
        pl.semaphore_signal(barrier, inc=1, device_id=to, device_id_type=MESH)

    def greet_loop(n, peer):
        def body(d, carry):
            greet(peer(d))
            return carry

        lax.fori_loop(1, n, body, 0)

    def f_copy(r):
        rows = pl.ds(pl.multiple_of(r * RB, RB), RB)
        return pltpu.make_async_copy(f_hbm.at[rows], f_v.at[rows], f_sem.at[r])

    ins = []
    for c in range(NC):
        lanes = pl.ds(c * W, W)
        ins.append((k_hbm.at[0, :, lanes], kw_v.at[c, :, pl.ds(0, W)]))
        ins.append((k_hbm.at[2, :, lanes], kw_v.at[c, :, pl.ds(W, W)]))
    ins.append((k_hbm.at[1], k1_v))
    ins.append((mix_hbm, mix_v))
    ins.append((cot_hbm, cot_v))
    ins = [pltpu.make_async_copy(s, d, in_sem.at[i]) for i, (s, d) in enumerate(ins)]
    f_copy(0).start()
    ins[0].start()
    ins[1].start()
    for r in range(1, NR):
        f_copy(r).start()
    for copy in ins[2:]:
        copy.start()

    greet(sibling)
    greet(ahead)
    greet(behind)
    greet_loop(NY, y_peer)
    greet_loop(NZ, z_peer)
    greet_loop(NX, x_peer)

    def loop(n, body):
        def step(i, carry):
            body(i)
            return carry

        lax.fori_loop(0, n, step, 0)

    def rows_at(base, i, n):
        return pl.ds(pl.multiple_of(base + i * n, n), n)

    def activate(r):
        def body(i):
            rows = pl.ds(pl.multiple_of(r * RB + i * 16, 16), 16)
            gelu, slope = gelu_and_slope(f_v[rows, :].astype(F32))
            act_v[rows, :] = gelu.astype(BF)
            slope_v[rows, :] = slope

        loop(RB // 16, body)

    def tap_copies(c, r):
        rows = pl.ds(pl.multiple_of(r * RB, RB), RB)
        return (
            pltpu.make_async_remote_copy(
                src_ref=t0_v.at[c, rows], dst_ref=te_v.at[c, rows],
                send_sem=halo_send.at[0], recv_sem=tap_recv.at[0, c, r],
                device_id=ahead, device_id_type=MESH,
            ),
            pltpu.make_async_remote_copy(
                src_ref=t2_v.at[c, rows], dst_ref=tl_v.at[c, rows],
                send_sem=halo_send.at[1], recv_sem=tap_recv.at[1, c, r],
                device_id=behind, device_id_type=MESH,
            ),
        )

    def taps(c, r):
        rows = pl.ds(pl.multiple_of(r * RB, RB), RB)
        both = nn(act_v[rows, :], kw_v[c]).astype(BF)
        t0_v[c, rows, :] = both[:, :W]
        t2_v[c, rows, :] = both[:, W:]

    def send_taps(c, r):
        for copy in tap_copies(c, r):
            copy.start()

    f_copy(0).wait()
    activate(0)
    ins[0].wait()
    ins[1].wait()
    taps(0, 0)
    pl.semaphore_wait(barrier, 1 + 2 + (NY - 1) + (NZ - 1) + (NX - 1))
    send_taps(0, 0)

    def first(i):
        r = i + 1
        f_copy(r).wait()
        activate(r)
        taps(0, r)
        send_taps(0, r)

    loop(NR - 1, first)
    for c in range(1, NC):
        ins[2 * c].wait()
        ins[2 * c + 1].wait()

        def more(r, c=c):
            taps(c, r)
            send_taps(c, r)

        loop(NR, more)

    for copy in ins[2 * NC:]:
        copy.wait()

    def own(r):
        rows = pl.ds(pl.multiple_of(r * RB, RB), RB)
        pre_v[rows, :] = nn(act_v[rows, :], k1_v[...]) + off_ref[...]
        hg_v[rows, :] = nt(cot_v[rows, :], mix_v[...])

    loop(NR, own)

    def pg_copies(c, r):
        rows = pl.ds(pl.multiple_of(r * RB, RB), RB)
        src = pg_v.at[rows, pl.ds(c * W, W)]
        return (
            pltpu.make_async_remote_copy(
                src_ref=src, dst_ref=pg02_v.at[c, rows, pl.ds(0, W)],
                send_sem=halo_send.at[2], recv_sem=pg_recv.at[0, c, r],
                device_id=behind, device_id_type=MESH,
            ),
            pltpu.make_async_remote_copy(
                src_ref=src, dst_ref=pg02_v.at[c, rows, pl.ds(W, W)],
                send_sem=halo_send.at[3], recv_sem=pg_recv.at[1, c, r],
                device_id=ahead, device_id_type=MESH,
            ),
        )

    def hidden(c):
        lanes = slice(c * W, (c + 1) * W)

        def block(r):
            for copy in tap_copies(c, r):
                copy.wait_recv()

            def body(i):
                rows = pl.ds(pl.multiple_of(r * RB + i * 64, 64), 64)
                pre = pre_v[rows, lanes] + te_v[c, rows, :].astype(F32) + tl_v[c, rows, :].astype(F32)
                gelu, slope = gelu_and_slope(pre)
                hid_v[rows, lanes] = gelu.astype(BF)
                pg_v[rows, lanes] = (hg_v[rows, lanes] * slope).astype(BF)

            loop(RB // 64, body)
            for copy in pg_copies(c, r):
                copy.start()

        loop(NR, block)

    CORE, Y, Z, X, GZ, GY, GC = range(7)

    def place(s):
        at, n = SEGS[s]
        half, quarter, part = n // 2, n // 8, n // 64
        own_half = at + core * half
        own_quarter = own_half + y * quarter
        own_part = own_quarter + z * part
        return at, half, quarter, part, own_half, own_quarter, own_part

    def ds(base, n):
        return pl.ds(pl.multiple_of(base, 16), n)

    def send(s, stage, src, dst, to):
        pltpu.make_async_remote_copy(
            src_ref=src, dst_ref=dst, send_sem=seg_send.at[s, stage], recv_sem=seg_recv.at[s, stage],
            device_id=to, device_id_type=MESH,
        ).start()

    def total(s, stage, ref):
        return pltpu.make_async_remote_copy(
            src_ref=ref, dst_ref=ref, send_sem=seg_send.at[s, stage], recv_sem=seg_recv.at[s, stage],
            device_id=sibling, device_id_type=MESH,
        )

    def bulk(s, stage):
        at, half, quarter, part, *_ = place(s)
        if stage in (CORE, GC):
            return rbc.at[pl.ds(at // 2, half)]
        if stage in (Y, GY):
            return rby.at[pl.ds(at // 8 * 3, 3 * quarter)]
        if stage in (Z, GZ):
            return rbz.at[pl.ds(at // 64 * 7, 7 * part)]
        return rbx.at[pl.ds(at // 64 * 4, 3 * part)]

    def core_send(s):
        at, half, *_ = place(s)
        other = at + (1 - core) * half

        def body(i):
            sbc[pl.ds(pl.multiple_of(at // 2 + i * 128, 128), 128), :] = g_v[
                ds(other + i * 128, 128), :
            ].astype(BF)

        loop(half // 128, body)
        rows = pl.ds(at // 2, half)
        send(s, CORE, sbc.at[rows], rbc.at[rows], sibling)

    def y_send(s):
        at, half, quarter, part, own_half, own_quarter, own_part = place(s)
        total(s, CORE, bulk(s, CORE)).wait_recv()

        def body(i):
            rows = ds(own_half + i * 128, 128)
            got = pl.ds(pl.multiple_of(at // 2 + i * 128, 128), 128)
            summed = g_v[rows, :] + rbc[got, :].astype(F32)
            g_v[rows, :] = summed
            sby[got, :] = summed.astype(BF)

        loop(half // 128, body)

        def to(d, carry):
            ty = lax.rem(y + d, NY)
            send(
                s, Y, sby.at[ds(at // 2 + ty * quarter, quarter)],
                rby.at[ds(at // 8 * 3 + (d - 1) * quarter, quarter)], y_peer(d),
            )
            return carry

        lax.fori_loop(1, NY, to, 0)

    def z_send(s):
        at, half, quarter, part, own_half, own_quarter, own_part = place(s)
        total(s, Y, bulk(s, Y)).wait_recv()

        def body(i):
            rows = ds(own_quarter + i * 64, 64)
            summed = g_v[rows, :]
            for d in range(NY - 1):
                summed = summed + rby[ds(at // 8 * 3 + d * quarter + i * 64, 64), :].astype(F32)
            g_v[rows, :] = summed
            sbz[ds(at // 8 + i * 64, 64), :] = summed.astype(BF)

        loop(quarter // 64, body)

        def to(d, carry):
            tz = lax.rem(z + d, NZ)
            send(
                s, Z, sbz.at[ds(at // 8 + tz * part, part)],
                rbz.at[ds(at // 64 * 7 + (d - 1) * part, part)], z_peer(d),
            )
            return carry

        lax.fori_loop(1, NZ, to, 0)

    def x_send(s):
        at, half, quarter, part, own_half, own_quarter, own_part = place(s)
        total(s, Z, bulk(s, Z)).wait_recv()
        summed = g_v[ds(own_part, part), :]
        for d in range(NZ - 1):
            summed = summed + rbz[ds(at // 64 * 7 + d * part, part), :].astype(F32)
        mine = rbx.at[ds(at // 64 * 4 + x * part, part)]
        sbx[pl.ds(at // 64, part), :] = summed.astype(BF)
        rbx[ds(at // 64 * 4 + x * part, part), :] = summed.astype(BF)

        def to(d, carry):
            send(s, X, sbx.at[pl.ds(at // 64, part)], mine, x_peer(d))
            return carry

        lax.fori_loop(1, NX, to, 0)

    def z_gather(s):
        at, half, quarter, part, own_half, own_quarter, own_part = place(s)
        total(s, X, bulk(s, X)).wait_recv()
        summed = rbx[pl.ds(at // 64 * 4, part), :].astype(F32)
        for k in range(1, NX):
            summed = summed + rbx[pl.ds(at // 64 * 4 + k * part, part), :].astype(F32)
        gg_v[ds(own_part, part), :] = summed.astype(BF)
        ref = gg_v.at[ds(own_part, part)]

        def to(d, carry):
            send(s, GZ, ref, ref, z_peer(d))
            return carry

        lax.fori_loop(1, NZ, to, 0)

    def y_gather(s):
        at, half, quarter, part, own_half, own_quarter, own_part = place(s)
        total(s, GZ, bulk(s, GZ)).wait_recv()
        ref = gg_v.at[ds(own_quarter, quarter)]

        def to(d, carry):
            send(s, GY, ref, ref, y_peer(d))
            return carry

        lax.fori_loop(1, NY, to, 0)

    def core_gather(s):
        at, half, quarter, part, own_half, own_quarter, own_part = place(s)
        total(s, GY, bulk(s, GY)).wait_recv()
        ref = gg_v.at[ds(own_half, half)]
        send(s, GC, ref, ref, sibling)

    def out_copy(s):
        at, n = SEGS[s]
        rows = pl.ds(at, n)
        return pltpu.make_async_copy(gg_v.at[rows], gg_hbm.at[rows], out_sem.at[2 + s])

    def finish(s):
        total(s, GC, bulk(s, GC)).wait_recv()
        out_copy(s).start()

    vec_stages = ((vc, 2, core, lambda d: sibling), (vy, NY, y, y_peer), (vz, NZ, z, z_peer), (vx, NX, x, x_peer))

    def vec_all(stage):
        ref, n, _, _ = vec_stages[stage]
        whole = ref.at[pl.ds(0, n - 1)]
        return pltpu.make_async_remote_copy(
            src_ref=whole, dst_ref=whole, send_sem=vec_send.at[stage], recv_sem=vec_recv.at[stage],
            device_id=sibling, device_id_type=MESH,
        )

    def vec_step(stage):
        if stage == 0:
            value = vs[0]
        else:
            vec_all(stage - 1).wait_recv()
            before, n, _, _ = vec_stages[stage - 1]
            value = before[0]
            for k in range(1, n):
                value = value + before[k]
        if stage == len(vec_stages):
            vec_ref[...] = value
            return
        ref, n, me, peer = vec_stages[stage]
        vs[stage] = value
        ref[me] = value

        def to(d, carry):
            pltpu.make_async_remote_copy(
                src_ref=vs.at[stage], dst_ref=ref.at[me],
                send_sem=vec_send.at[stage], recv_sem=vec_recv.at[stage],
                device_id=peer(d), device_id_type=MESH,
            ).start()
            return carry

        lax.fori_loop(1, n, to, 0)

    def transpose(r):
        for r in range(NR):
            rows = pl.ds(r * RB, RB)
            actt_v[:, rows] = act_v[rows, :].T

    hidden(0)
    transpose(0)
    hidden(1)
    hidden(2)

    for r in range(NR):
        rows = pl.ds(r * RB, RB)
        hidt_v[:, rows] = hid_v[rows, :].T

    def kg1(m):
        part = nn(actt_v[pl.ds(pl.multiple_of(m * 256, 256), 256), :], pg_v[...])
        for c in range(NC):
            g_v[pl.ds(pl.multiple_of(KG1_AT + c * C + m * 256, 256), 256), :] = part[:, c * W:(c + 1) * W]

    loop(C // 256, kg1)
    for j in range(C // 256):
        part = nn(hidt_v[...], cot_v[:, j * 256:(j + 1) * 256])
        for c in range(H // W):
            for k in range(2):
                at = MG_AT + (c * (C // W) + j * 2 + k) * W
                g_v[pl.ds(at, W), :] = part[c * W:(c + 1) * W, k * W:(k + 1) * W]

    core_send(0)
    ones = jnp.ones((8, ROWS), BF)
    cot_sum = nn(ones, cot_v[...])
    pg_sum = nn(ones, pg_v[...])
    for j in range(C // W):
        vs[0, j:j + 1, :] = cot_sum[:1, j * W:(j + 1) * W]
    for j in range(H // W):
        vs[0, C // W + j:C // W + j + 1, :] = pg_sum[:1, j * W:(j + 1) * W]
    done = C // W + H // W
    vs[0, done:, :] = jnp.zeros((VEC - done, W), F32)
    vec_step(0)

    def kg02(c):
        def wait(r):
            for copy in pg_copies(c, r):
                copy.wait_recv()

        loop(NR, wait)

        def block(m):
            part = nn(actt_v[pl.ds(pl.multiple_of(m * 256, 256), 256), :], pg02_v[c])
            at = KG02_AT + c * 2 * C + m * 256
            g_v[pl.ds(pl.multiple_of(at, 256), 256), :] = part[:, :W]
            g_v[pl.ds(pl.multiple_of(at + C, 256), 256), :] = part[:, W:]

        loop(C // 256, block)

    def leave(r):
        rows = pl.ds(pl.multiple_of(r * RB, RB), RB)
        lo_v[rows, :] = (f_v[rows, :].astype(F32) + nn(hid_v[rows, :], mix_v[...]) + bias_ref[...]).astype(BF)

    y_send(0)
    vec_step(1)
    loop(NR, leave)
    lo_copy = pltpu.make_async_copy(lo_v, lo_hbm, out_sem.at[0])
    lo_copy.start()
    kg02(0)
    core_send(1)
    z_send(0)
    vec_step(2)
    y_send(1)
    x_send(0)
    vec_step(3)
    kg02(1)
    core_send(2)
    z_gather(0)
    vec_step(4)
    z_send(1)
    y_send(2)
    kg02(2)
    core_send(3)
    y_gather(0)
    x_send(1)
    z_send(2)
    y_send(3)

    def grad_in(r):
        rows = pl.ds(pl.multiple_of(r * RB, RB), RB)
        grad = nt(pg_v[rows, :], k1_v[...])
        for c in range(NC):
            grad = grad + nt(pg02_v[c, rows, :], kw_v[c])
        ig_v[rows, :] = (cot_v[rows, :].astype(F32) + grad * slope_v[rows, :]).astype(BF)

    loop(2, grad_in)
    core_gather(0)
    z_gather(1)
    x_send(2)
    z_send(3)
    loop(2, lambda i: grad_in(i + 2))
    ig_copy = pltpu.make_async_copy(ig_v, ig_hbm, out_sem.at[1])
    ig_copy.start()
    y_gather(1)
    z_gather(2)
    x_send(3)
    finish(0)
    core_gather(1)
    y_gather(2)
    z_gather(3)
    finish(1)
    core_gather(2)
    y_gather(3)
    finish(2)
    core_gather(3)
    finish(3)

    for d, ref in ((0, t0_v), (1, t2_v), (2, t0_v), (3, t2_v)):
        pltpu.make_async_remote_copy(
            src_ref=ref, dst_ref=ref, send_sem=halo_send.at[d], recv_sem=tap_recv.at[0, 0, 0],
            device_id=sibling, device_id_type=MESH,
        ).wait_send()
    for stage in range(len(vec_stages)):
        vec_all(stage).wait_send()
    for s in range(len(SEGS)):
        for stage in range(7):
            total(s, stage, bulk(s, stage)).wait_send()
    lo_copy.wait()
    ig_copy.wait()
    for s in range(len(SEGS)):
        out_copy(s).wait()


def finish_kernel(factor, lo_in, ig_in, gg_in, lo_out, ig_out, kg_out, mg_out, gg_v, kg_v, mg_v, sem):
    copies = [
        pltpu.make_async_copy(lo_in, lo_out, sem.at[0]),
        pltpu.make_async_copy(ig_in, ig_out, sem.at[1]),
    ]
    load = [
        pltpu.make_async_copy(
            gg_in.at[pl.ds(at, n)], gg_v.at[pl.ds(at, n)], sem.at[2 + i]
        )
        for i, (at, n) in enumerate(((KG1_AT, NC * C), (MG_AT, NC * C), (KG02_AT, 2 * NC * C)))
    ]
    for copy in load + copies:
        copy.start()
    stores = [pltpu.make_async_copy(kg_v.at[k], kg_out.at[k], sem.at[5 + k]) for k in range(3)]
    stores.append(pltpu.make_async_copy(mg_v, mg_out, sem.at[8]))

    def spread(k, starts):
        for c in range(NC):
            def body(i, carry, c=c):
                rows = pl.ds(pl.multiple_of(i * 128, 128), 128)
                source = pl.ds(pl.multiple_of(starts[c] + i * 128, 128), 128)
                kg_v[k, rows, c * W:(c + 1) * W] = gg_v[source, :].astype(F32) * factor
                return carry

            lax.fori_loop(0, C // 128, body, 0)
        stores[k].start()

    load[0].wait()
    spread(1, [KG1_AT + c * C for c in range(NC)])
    load[1].wait()
    for c in range(H // W):
        for j in range(C // W):
            at = MG_AT + (c * (C // W) + j) * W
            mg_v[c * W:(c + 1) * W, j * W:(j + 1) * W] = gg_v[at:at + W, :].astype(F32) * factor
    stores[3].start()
    load[2].wait()
    spread(0, [KG02_AT + c * 2 * C for c in range(NC)])
    spread(2, [KG02_AT + c * 2 * C + C for c in range(NC)])
    for copy in copies + stores:
        copy.wait()


def local(features, kernel, offsets, mixer, biases, cotangent):
    length = features.shape[0] * lax.axis_size("seq") * lax.axis_size("sub")
    factor = 1.0 / math.sqrt(length)
    any_spec = pl.BlockSpec(memory_space=pl.ANY)
    vmem_spec = pl.BlockSpec(memory_space=pltpu.VMEM)
    n = len(SEGS)
    vm = pltpu.VMEM
    dma = pltpu.SemaphoreType.DMA
    lo, ig, gg, vec = pl.pallas_call(
        main_kernel,
        out_shape=(
            jax.ShapeDtypeStruct((ROWS, C), BF),
            jax.ShapeDtypeStruct((ROWS, C), BF),
            jax.ShapeDtypeStruct((TOTAL, W), BF),
            jax.ShapeDtypeStruct((VEC, W), F32),
        ),
        in_specs=[any_spec, any_spec, vmem_spec, any_spec, vmem_spec, any_spec],
        out_specs=(any_spec, any_spec, any_spec, vmem_spec),
        scratch_shapes=[
            vm((ROWS, C), BF), vm((ROWS, C), BF), vm((NC, C, 2 * W), BF), vm((C, H), BF), vm((H, C), BF),
            vm((ROWS, C), BF), vm((C, ROWS), BF), vm((ROWS, C), F32), vm((ROWS, H), F32), vm((ROWS, H), F32),
            vm((NC, ROWS, W), BF), vm((NC, ROWS, W), BF), vm((NC, ROWS, W), BF), vm((NC, ROWS, W), BF),
            vm((ROWS, H), BF), vm((H, ROWS), BF), vm((ROWS, H), BF), vm((NC, ROWS, 2 * W), BF),
            vm((ROWS, C), BF), vm((ROWS, C), BF), vm((TOTAL, W), F32),
            vm((TOTAL // 2, W), BF), vm((TOTAL // 2, W), BF), vm((TOTAL // 2, W), BF), vm((TOTAL // 8 * 3, W), BF),
            vm((TOTAL // 8, W), BF), vm((TOTAL // 64 * 7, W), BF), vm((TOTAL // 64, W), BF),
            vm((TOTAL // 64 * 4, W), BF), vm((TOTAL, W), BF),
            vm((4, VEC, W), F32), vm((2, VEC, W), F32), vm((NY, VEC, W), F32), vm((NZ, VEC, W), F32),
            vm((NX, VEC, W), F32),
            dma((NR,)), dma((2 * NC + 3,)), dma((2 + n,)), dma((4,)), dma((2, NC, NR)), dma((2, NC, NR)),
            dma((n, 7)), dma((n, 7)), dma((4,)), dma((4,)),
        ],
        compiler_params=pltpu.CompilerParams(
            collective_id=0, has_side_effects=True, vmem_limit_bytes=60 * 2**20
        ),
        cost_estimate=pl.CostEstimate(flops=8_000_000_000, bytes_accessed=16_000_000, transcendentals=1_200_000),
        name="block",
    )(features, kernel, offsets.reshape(1, H), mixer, biases.reshape(1, C), cotangent)
    layer_output, input_grad, kernel_grad, mixer_grad = pl.pallas_call(
        lambda *refs: finish_kernel(factor, *refs),
        out_shape=(
            jax.ShapeDtypeStruct((ROWS, C), BF),
            jax.ShapeDtypeStruct((ROWS, C), BF),
            jax.ShapeDtypeStruct((3, C, H), F32),
            jax.ShapeDtypeStruct((H, C), F32),
        ),
        in_specs=[any_spec] * 3,
        out_specs=(any_spec,) * 4,
        scratch_shapes=[vm((TOTAL, W), BF), vm((3, C, H), F32), vm((H, C), F32), dma((9,))],
        compiler_params=pltpu.CompilerParams(vmem_limit_bytes=24 * 2**20),
        name="finish",
    )(lo, ig, gg)
    sums = vec.reshape(VEC * W) * factor
    return (layer_output, input_grad, kernel_grad, sums[C:C + H], mixer_grad, sums[:C])


def solution(mesh):
    placed = (P(("seq", "sub"), None), P(), P(), P(), P(), P(("seq", "sub"), None))
    return jax.shard_map(
        local,
        mesh=mesh,
        in_specs=placed,
        out_specs=(P(("seq", "sub"), None), P(("seq", "sub"), None), P(), P(), P(), P()),
        check_vma=False,
    )
```

time: 359 us -> 106 us (0.30)
  waiting for transfers between devices: 213 us -> 0 us
  Pallas kernels: 0 us -> 96.7 us
  blocking collectives: 77.3 us -> 0 us
  matrix products: 21.4 us -> 0 us
  starting transfers between devices: 14.7 us -> 0 us
  between operations: 14.2 us -> 0.65 us
  other arithmetic: 10.4 us -> 0.7 us
    psum x1 -> x0, waiting for transfers between devices: 184 us -> none  [local(): lax.psum((kernel_part, offset_part, mixer_part, biases_part), ('seq', 'su...]
    pallas_call x0 -> x2, Pallas kernels: none -> 96.7 us  [the longest x1 93 us: local(): pl.pallas_call(main_kernel, out_shape=(jax.ShapeDtypeStruct((ROWS, C), BF...]
    psum x1 -> x0, blocking collectives: 77.3 us -> none  [local(): lax.psum((kernel_part, offset_part, mixer_part, biases_part), ('seq', 'su...]
    ppermute x4 -> x0, waiting for transfers between devices: 29.4 us -> none  [from_behind(): return lax.ppermute(value, axis, pairs)]
    dot_general x12 -> x0, matrix products: 21.4 us -> none  [the longest x4 8.21 us: times_transposed(): lax.dot_general(left, right, (((1,), (1,)), ((), ())), preferred_element_...]
    ppermute x4 -> x0, starting transfers between devices: 14.6 us -> none  [from_behind(): return lax.ppermute(value, axis, pairs)]
    convert_element_type x1 -> x0, other arithmetic: 8.04 us -> none  [local(): activated_output = gelu_exact(inputs).astype(jnp.bfloat16)]
  transfers between devices with their start and end apart: 5 -> 0, of which waited for: 3 -> 0; matrix products, arithmetic and copies ran while one was open for 4% -> 0% of each run, Pallas kernels for 0% -> 0%
where the time goes in v2:
time: 106 us
  Pallas kernels  96.7 us (91%)
  local copies, waits for them, and re-layouts  8.17 us (8%)
    pallas_call x1, Pallas kernels, local(): pl.pallas_call(main_kernel, out_shape=(jax.ShapeDtypeStruct((ROWS, C), BF...  93 us
    unnamed x6, local copies, waits for them, and re-layouts  4.48 us
    pallas_call x1, Pallas kernels, local(): pl.pallas_call(lambda *refs: finish_kernel(factor, *refs), out_shape=(jax...  3.7 us

profile of v2, /device:TPU:1, one launch (start us, length us, event | category | flops | bytes accessed | tf_op | source)
XLA Modules:
  0.0 106.2 jit_solution(14743096230264277543)
XLA Ops:
  0.6 1.2 %reshape.23.off_ref = f32[1,384]{1,0:T(1,128)} reshape(f32[384]{0:T(512)} %param.8) | data formatting | bytes 3072 | tf_op jit(solution)/shard_map/reshape | solution.py:653
  1.9 1.3 %reshape.24.bias_ref = f32[1,768]{1,0:T(1,128)} reshape(f32[768]{0:T(1024)} %param.10) | data formatting | bytes 6144 | tf_op jit(solution)/shard_map/reshape | solution.py:653
  3.1 93.0 %block.1 = (bf16[1024,768]{1,0:T(8,128)(2,1)}, bf16[1024,768]{1,0:T(8,128)(2,1)}, bf16[9216,128]{1,0:T(8,128)(2,1)}, f32[16,128]{1,0:T(8,128)}) custom-call(bf16[1024,768]{1,0:T(8,128)(2,1)} %f_hbm.1, bf16[3,768,384]{2,1,0:T(8,128)(2,1)} %k_hbm.1, f32[1,384]{1,0:T(1,128)} %reshape.23.off_ref, bf16[384,768]{1,0:T(8,128)(2,1)} %mix_hbm.1, ...), custom_call_target="tpu_custom_call" | custom-call | flops 8000000000 | bytes 16000000 | tf_op jit(solution)/shard_map/block/pallas_call | solution.py:624
  96.1 0.7 broadcast_multiply_fusion
  96.8 0.6 slice_bitcast_fusion.1
  97.4 0.6 slice_bitcast_fusion
  98.0 0.0 copy-start
  98.0 1.7 %copy-done = bf16[9216,128]{1,0:T(8,128)(2,1)S(1)} copy-done((bf16[9216,128]{1,0:T(8,128)(2,1)S(1)}, bf16[9216,128]{1,0:T(8,128)(2,1)}, u32[]{:S(2)}) %copy-start) | copy-done | bytes 2359320
  99.7 0.0 copy-start.1
  99.7 1.4 %copy-done.1 = bf16[1024,768]{1,0:T(8,128)(2,1)S(1)} copy-done((bf16[1024,768]{1,0:T(8,128)(2,1)S(1)}, bf16[1024,768]{1,0:T(8,128)(2,1)}, u32[]{:S(2)}) %copy-start.1) | copy-done | bytes 1572888
  101.1 0.0 copy-start.2
  101.1 1.4 %copy-done.2 = bf16[1024,768]{1,0:T(8,128)(2,1)S(1)} copy-done((bf16[1024,768]{1,0:T(8,128)(2,1)S(1)}, bf16[1024,768]{1,0:T(8,128)(2,1)}, u32[]{:S(2)}) %copy-start.2) | copy-done | bytes 1572888
  102.5 3.7 %finish.1 = (bf16[1024,768]{1,0:T(8,128)(2,1)}, bf16[1024,768]{1,0:T(8,128)(2,1)}, f32[3,768,384]{2,1,0:T(8,128)}, f32[384,768]{1,0:T(8,128)}) custom-call(bf16[1024,768]{1,0:T(8,128)(2,1)S(1)} %copy-done.1, bf16[1024,768]{1,0:T(8,128)(2,1)S(1)} %copy-done.2, bf16[9216,128]{1,0:T(8,128)(2,1)S(1)} %copy-done), custom_call_target="tpu_custom_call" | custom-call | tf_op jit(solution)/shard_map/finish/pallas_call | solution.py:654
Async XLA Ops:
  98.0 1.7 %copy-start = (bf16[9216,128]{1,0:T(8,128)(2,1)S(1)}, bf16[9216,128]{1,0:T(8,128)(2,1)}, u32[]{:S(2)}) copy-start(bf16[9216,128]{1,0:T(8,128)(2,1)} %get-tuple-element.16.refs_2_) | copy-start | bytes 7077892
  99.7 1.4 %copy-start.1 = (bf16[1024,768]{1,0:T(8,128)(2,1)S(1)}, bf16[1024,768]{1,0:T(8,128)(2,1)}, u32[]{:S(2)}) copy-start(bf16[1024,768]{1,0:T(8,128)(2,1)} %get-tuple-element.14.refs_0_) | copy-start | bytes 4718596
  101.1 1.4 %copy-start.2 = (bf16[1024,768]{1,0:T(8,128)(2,1)S(1)}, bf16[1024,768]{1,0:T(8,128)(2,1)}, u32[]{:S(2)}) copy-start(bf16[1024,768]{1,0:T(8,128)(2,1)} %get-tuple-element.15.refs_1_) | copy-start | bytes 4718596

commit v3 on v2

--- a/solution.py
+++ b/solution.py
@@ -22,11 +22,14 @@
 
 NX, NY, NZ = 4, 4, 8
 
-KG1_AT = 0
-MG_AT = NC * C
-KG02_AT = MG_AT + (H // W) * (C // W) * W
-TOTAL = KG02_AT + 2 * NC * C
-SEGS = ((0, 4096), (4096, 2048), (6144, 1024), (7168, 2048))
+PAIR = 2 * C
+KG1_AT, MG_AT, KG02_AT = 0, C, NC * PAIR
+TOTAL = 2 * NC * PAIR
+SEGS = ((0, 3072), (3072, 3072), (6144, 1024), (7168, 2048))
+LAST = len(SEGS) - 1
+NP = NX * NY
+SHARE = SEGS[LAST][1] // (2 * NP)
+SLICE = SHARE // NZ
 VEC = 16
 
 T_SCALE = 0.3
@@ -74,14 +77,15 @@
 
 
 def main_kernel(
-    f_hbm, k_hbm, off_ref, mix_hbm, bias_ref, cot_hbm,
-    lo_hbm, ig_hbm, gg_hbm, vec_ref,
-    f_v, cot_v, kw_v, k1_v, mix_v,
+    f_hbm, k_hbm, off_hbm, mix_hbm, bias_hbm, cot_hbm,
+    lo_v, ig_v, gg_v, vec_ref,
+    f_v, cot_v, kw_v, k1_v, mix_v, off_v, bias_v,
     act_v, actt_v, slope_v, pre_v, hg_v,
     t0_v, t2_v, te_v, tl_v, hid_v, hidt_v, pg_v, pg02_v,
-    lo_v, ig_v, g_v, sbc, rbc, sby, rby, sbz, rbz, sbx, rbx, gg_v,
+    g_v, sbc, rbc, sby, rby, sbz, rbz, sbx, rbx,
+    last_s, last_r, last_own, last_zs, last_zr, last_g,
     vs, vc, vy, vz, vx,
-    f_sem, in_sem, out_sem, halo_send, tap_recv, pg_recv, seg_send, seg_recv, vec_send, vec_recv,
+    f_sem, in_sem, halo_send, tap_recv, pg_recv, seg_send, seg_recv, vec_send, vec_recv,
 ):
     seq, sub, x, y, z, core = position()
     nseq = 2 * NX * NZ
@@ -96,6 +100,12 @@
 
     def x_peer(d):
         return device(lax.rem(x + d, NX), y, z, core)
+
+    def xy_at(d):
+        return lax.rem(x * NY + y + d, NP)
+
+    def xy_peer(d):
+        return device(lax.div(xy_at(d), NY), lax.rem(xy_at(d), NY), z, core)
 
     sibling = device(x, y, z, 1 - core)
 
@@ -123,6 +133,8 @@
     ins.append((k_hbm.at[1], k1_v))
     ins.append((mix_hbm, mix_v))
     ins.append((cot_hbm, cot_v))
+    ins.append((off_hbm, off_v))
+    ins.append((bias_hbm, bias_v))
     ins = [pltpu.make_async_copy(s, d, in_sem.at[i]) for i, (s, d) in enumerate(ins)]
     f_copy(0).start()
     ins[0].start()
@@ -135,9 +147,8 @@
     greet(sibling)
     greet(ahead)
     greet(behind)
-    greet_loop(NY, y_peer)
+    greet_loop(NP, xy_peer)
     greet_loop(NZ, z_peer)
-    greet_loop(NX, x_peer)
 
     def loop(n, body):
         def step(i, carry):
@@ -183,12 +194,14 @@
         for copy in tap_copies(c, r):
             copy.start()
 
-    f_copy(0).wait()
-    activate(0)
-    ins[0].wait()
-    ins[1].wait()
-    taps(0, 0)
-    pl.semaphore_wait(barrier, 1 + 2 + (NY - 1) + (NZ - 1) + (NX - 1))
+    with jax.named_scope("start"):
+        f_copy(0).wait()
+        activate(0)
+        ins[0].wait()
+        ins[1].wait()
+        taps(0, 0)
+    with jax.named_scope("greeted"):
+        pl.semaphore_wait(barrier, 1 + 2 + (NP - 1) + (NZ - 1))
     send_taps(0, 0)
 
     def first(i):
@@ -198,7 +211,8 @@
         taps(0, r)
         send_taps(0, r)
 
-    loop(NR - 1, first)
+    with jax.named_scope("first"):
+        loop(NR - 1, first)
     for c in range(1, NC):
         ins[2 * c].wait()
         ins[2 * c + 1].wait()
@@ -207,17 +221,19 @@
             taps(c, r)
             send_taps(c, r)
 
-        loop(NR, more)
+        with jax.named_scope("more_taps"):
+            loop(NR, more)
 
     for copy in ins[2 * NC:]:
         copy.wait()
 
     def own(r):
         rows = pl.ds(pl.multiple_of(r * RB, RB), RB)
-        pre_v[rows, :] = nn(act_v[rows, :], k1_v[...]) + off_ref[...]
+        pre_v[rows, :] = nn(act_v[rows, :], k1_v[...]) + off_v[...].reshape(1, H)
         hg_v[rows, :] = nt(cot_v[rows, :], mix_v[...])
 
-    loop(NR, own)
+    with jax.named_scope("own"):
+        loop(NR, own)
 
     def pg_copies(c, r):
         rows = pl.ds(pl.multiple_of(r * RB, RB), RB)
@@ -235,7 +251,7 @@
             ),
         )
 
-    def hidden(c):
+    def hidden(c, first=0, last=NR):
         lanes = slice(c * W, (c + 1) * W)
 
         def block(r):
@@ -253,7 +269,7 @@
             for copy in pg_copies(c, r):
                 copy.start()
 
-        loop(NR, block)
+        loop(last - first, lambda i: block(first + i))
 
     CORE, Y, Z, X, GZ, GY, GC = range(7)
 
@@ -282,6 +298,10 @@
 
     def bulk(s, stage):
         at, half, quarter, part, *_ = place(s)
+        if s == LAST and stage in (Y, GY):
+            return last_r
+        if s == LAST and stage in (Z, GZ):
+            return last_zr
         if stage in (CORE, GC):
             return rbc.at[pl.ds(at // 2, half)]
         if stage in (Y, GY):
@@ -398,14 +418,70 @@
         ref = gg_v.at[ds(own_half, half)]
         send(s, GC, ref, ref, sibling)
 
-    def out_copy(s):
-        at, n = SEGS[s]
-        rows = pl.ds(at, n)
-        return pltpu.make_async_copy(gg_v.at[rows], gg_hbm.at[rows], out_sem.at[2 + s])
+    last_half = SEGS[LAST][0] + core * (SEGS[LAST][1] // 2)
+
+    def last_xy():
+        at, half, *_ = place(LAST)
+        total(LAST, CORE, bulk(LAST, CORE)).wait_recv()
+
+        def body(i):
+            rows = ds(last_half + i * SHARE, SHARE)
+            got = pl.ds(pl.multiple_of(at // 2 + i * SHARE, SHARE), SHARE)
+            summed = g_v[rows, :] + rbc[got, :].astype(F32)
+            g_v[rows, :] = summed
+            last_s[i] = summed.astype(BF)
+
+        loop(NP, body)
+
+        def to(d, carry):
+            send(LAST, Y, last_s.at[xy_at(d)], last_r.at[d - 1], xy_peer(d))
+            return carry
+
+        lax.fori_loop(1, NP, to, 0)
+
+    def last_z():
+        total(LAST, Y, last_r).wait_recv()
+        summed = g_v[ds(last_half + xy_at(0) * SHARE, SHARE), :]
+        for d in range(NP - 1):
+            summed = summed + last_r[d].astype(F32)
+        summed = summed.reshape(NZ, SLICE, W)
+        last_own[...] = summed
+        last_zs[...] = summed.astype(BF)
+
+        def to(d, carry):
+            send(LAST, Z, last_zs.at[lax.rem(z + d, NZ)], last_zr.at[d - 1], z_peer(d))
+            return carry
+
+        lax.fori_loop(1, NZ, to, 0)
+
+    def last_z_gather():
+        total(LAST, Z, last_zr).wait_recv()
+        summed = last_own[z]
+        for d in range(NZ - 1):
+            summed = summed + last_zr[d].astype(F32)
+        last_g[z] = summed.astype(BF)
+        ref = last_g.at[z]
+
+        def to(d, carry):
+            send(LAST, GZ, ref, ref, z_peer(d))
+            return carry
+
+        lax.fori_loop(1, NZ, to, 0)
+
+    def last_xy_gather():
+        total(LAST, GZ, last_zr).wait_recv()
+        rows = ds(last_half + xy_at(0) * SHARE, SHARE)
+        gg_v[rows, :] = last_g[...].astype(F32).reshape(SHARE, W).astype(BF)
+        ref = gg_v.at[rows]
+
+        def to(d, carry):
+            send(LAST, GY, ref, ref, xy_peer(d))
+            return carry
+
+        lax.fori_loop(1, NP, to, 0)
 
     def finish(s):
         total(s, GC, bulk(s, GC)).wait_recv()
-        out_copy(s).start()
 
     vec_stages = ((vc, 2, core, lambda d: sibling), (vy, NY, y, y_peer), (vz, NZ, z, z_peer), (vx, NX, x, x_peer))
 
@@ -448,39 +524,36 @@
             rows = pl.ds(r * RB, RB)
             actt_v[:, rows] = act_v[rows, :].T
 
-    hidden(0)
-    transpose(0)
-    hidden(1)
-    hidden(2)
-
-    for r in range(NR):
-        rows = pl.ds(r * RB, RB)
-        hidt_v[:, rows] = hid_v[rows, :].T
-
-    def kg1(m):
-        part = nn(actt_v[pl.ds(pl.multiple_of(m * 256, 256), 256), :], pg_v[...])
-        for c in range(NC):
-            g_v[pl.ds(pl.multiple_of(KG1_AT + c * C + m * 256, 256), 256), :] = part[:, c * W:(c + 1) * W]
-
-    loop(C // 256, kg1)
-    for j in range(C // 256):
-        part = nn(hidt_v[...], cot_v[:, j * 256:(j + 1) * 256])
-        for c in range(H // W):
-            for k in range(2):
-                at = MG_AT + (c * (C // W) + j * 2 + k) * W
-                g_v[pl.ds(at, W), :] = part[c * W:(c + 1) * W, k * W:(k + 1) * W]
-
-    core_send(0)
-    ones = jnp.ones((8, ROWS), BF)
-    cot_sum = nn(ones, cot_v[...])
-    pg_sum = nn(ones, pg_v[...])
-    for j in range(C // W):
-        vs[0, j:j + 1, :] = cot_sum[:1, j * W:(j + 1) * W]
-    for j in range(H // W):
-        vs[0, C // W + j:C // W + j + 1, :] = pg_sum[:1, j * W:(j + 1) * W]
-    done = C // W + H // W
-    vs[0, done:, :] = jnp.zeros((VEC - done, W), F32)
-    vec_step(0)
+    def kg1_and_mixer(c, n):
+        lanes = slice(c * W, (c + n) * W)
+        for r in range(NR):
+            rows = pl.ds(r * RB, RB)
+            hidt_v[lanes, rows] = hid_v[rows, lanes].T
+
+        def kg1(m):
+            part = nn(actt_v[pl.ds(pl.multiple_of(m * 256, 256), 256), :], pg_v[:, lanes])
+            for k in range(n):
+                at = KG1_AT + (c + k) * PAIR + m * 256
+                g_v[pl.ds(pl.multiple_of(at, 256), 256), :] = part[:, k * W:(k + 1) * W]
+
+        loop(C // 256, kg1)
+        for j in range(C // 256):
+            part = nn(hidt_v[lanes, :], cot_v[:, j * 256:(j + 1) * 256])
+            for i in range(n):
+                for k in range(2):
+                    at = MG_AT + (c + i) * PAIR + (j * 2 + k) * W
+                    g_v[pl.ds(at, W), :] = part[i * W:(i + 1) * W, k * W:(k + 1) * W]
+
+    def vectors():
+        ones = jnp.ones((8, ROWS), BF)
+        cot_sum = nn(ones, cot_v[...])
+        pg_sum = nn(ones, pg_v[...])
+        for j in range(C // W):
+            vs[0, j:j + 1, :] = cot_sum[:1, j * W:(j + 1) * W]
+        for j in range(H // W):
+            vs[0, C // W + j:C // W + j + 1, :] = pg_sum[:1, j * W:(j + 1) * W]
+        done = C // W + H // W
+        vs[0, done:, :] = jnp.zeros((VEC - done, W), F32)
 
     def kg02(c):
         def wait(r):
@@ -491,7 +564,7 @@
 
         def block(m):
             part = nn(actt_v[pl.ds(pl.multiple_of(m * 256, 256), 256), :], pg02_v[c])
-            at = KG02_AT + c * 2 * C + m * 256
+            at = KG02_AT + c * PAIR + m * 256
             g_v[pl.ds(pl.multiple_of(at, 256), 256), :] = part[:, :W]
             g_v[pl.ds(pl.multiple_of(at + C, 256), 256), :] = part[:, W:]
 
@@ -499,32 +572,7 @@
 
     def leave(r):
         rows = pl.ds(pl.multiple_of(r * RB, RB), RB)
-        lo_v[rows, :] = (f_v[rows, :].astype(F32) + nn(hid_v[rows, :], mix_v[...]) + bias_ref[...]).astype(BF)
-
-    y_send(0)
-    vec_step(1)
-    loop(NR, leave)
-    lo_copy = pltpu.make_async_copy(lo_v, lo_hbm, out_sem.at[0])
-    lo_copy.start()
-    kg02(0)
-    core_send(1)
-    z_send(0)
-    vec_step(2)
-    y_send(1)
-    x_send(0)
-    vec_step(3)
-    kg02(1)
-    core_send(2)
-    z_gather(0)
-    vec_step(4)
-    z_send(1)
-    y_send(2)
-    kg02(2)
-    core_send(3)
-    y_gather(0)
-    x_send(1)
-    z_send(2)
-    y_send(3)
+        lo_v[rows, :] = (f_v[rows, :].astype(F32) + nn(hid_v[rows, :], mix_v[...]) + bias_v[...].reshape(1, C)).astype(BF)
 
     def grad_in(r):
         rows = pl.ds(pl.multiple_of(r * RB, RB), RB)
@@ -533,27 +581,57 @@
             grad = grad + nt(pg02_v[c, rows, :], kw_v[c])
         ig_v[rows, :] = (cot_v[rows, :].astype(F32) + grad * slope_v[rows, :]).astype(BF)
 
-    loop(2, grad_in)
+    hidden(0)
+    transpose(0)
+    hidden(1)
+    kg1_and_mixer(0, 2)
+    core_send(0)
+    hidden(2, 0, 2)
+    y_send(0)
+    hidden(2, 2, NR)
+    kg1_and_mixer(2, 1)
+    vectors()
+    vec_step(0)
+    loop(2, leave)
+    z_send(0)
+    loop(2, lambda i: leave(i + 2))
+    kg02(0)
+    core_send(1)
+    vec_step(1)
+    y_send(1)
+    x_send(0)
+    kg02(1)
+    core_send(2)
+    z_gather(0)
+    y_send(2)
+    vec_step(2)
+    z_send(1)
+    kg02(2)
+    core_send(LAST)
+    z_send(2)
+    y_gather(0)
+    last_xy()
+    x_send(1)
+    x_send(2)
+    z_gather(1)
+    grad_in(0)
     core_gather(0)
-    z_gather(1)
-    x_send(2)
-    z_send(3)
-    loop(2, lambda i: grad_in(i + 2))
-    ig_copy = pltpu.make_async_copy(ig_v, ig_hbm, out_sem.at[1])
-    ig_copy.start()
+    z_gather(2)
+    last_z()
+    vec_step(3)
+    grad_in(1)
     y_gather(1)
-    z_gather(2)
-    x_send(3)
-    finish(0)
+    last_z_gather()
+    y_gather(2)
+    grad_in(2)
+    last_xy_gather()
+    grad_in(3)
     core_gather(1)
-    y_gather(2)
-    z_gather(3)
-    finish(1)
     core_gather(2)
-    y_gather(3)
-    finish(2)
-    core_gather(3)
-    finish(3)
+    vec_step(4)
+    core_gather(LAST)
+    for s in range(len(SEGS)):
+        finish(s)
 
     for d, ref in ((0, t0_v), (1, t2_v), (2, t0_v), (3, t2_v)):
         pltpu.make_async_remote_copy(
@@ -564,59 +642,51 @@
         vec_all(stage).wait_send()
     for s in range(len(SEGS)):
         for stage in range(7):
-            total(s, stage, bulk(s, stage)).wait_send()
-    lo_copy.wait()
-    ig_copy.wait()
-    for s in range(len(SEGS)):
-        out_copy(s).wait()
-
-
-def finish_kernel(factor, lo_in, ig_in, gg_in, lo_out, ig_out, kg_out, mg_out, gg_v, kg_v, mg_v, sem):
-    copies = [
-        pltpu.make_async_copy(lo_in, lo_out, sem.at[0]),
-        pltpu.make_async_copy(ig_in, ig_out, sem.at[1]),
+            if s != LAST or stage != X:
+                total(s, stage, bulk(s, stage)).wait_send()
+
+
+def finish_kernel(
+    factor, lo_v, ig_v, gg_v, vec_in, lo_out, ig_out, kg_out, mg_out, offset_out, biases_out, kg_v, mg_v, sem
+):
+    stores = [
+        pltpu.make_async_copy(lo_v, lo_out, sem.at[0]),
+        pltpu.make_async_copy(ig_v, ig_out, sem.at[1]),
+        pltpu.make_async_copy(mg_v, mg_out, sem.at[2]),
     ]
-    load = [
-        pltpu.make_async_copy(
-            gg_in.at[pl.ds(at, n)], gg_v.at[pl.ds(at, n)], sem.at[2 + i]
-        )
-        for i, (at, n) in enumerate(((KG1_AT, NC * C), (MG_AT, NC * C), (KG02_AT, 2 * NC * C)))
-    ]
-    for copy in load + copies:
-        copy.start()
-    stores = [pltpu.make_async_copy(kg_v.at[k], kg_out.at[k], sem.at[5 + k]) for k in range(3)]
-    stores.append(pltpu.make_async_copy(mg_v, mg_out, sem.at[8]))
-
-    def spread(k, starts):
+    stores += [pltpu.make_async_copy(kg_v.at[k], kg_out.at[k], sem.at[3 + k]) for k in range(3)]
+
+    def spread(k, start):
         for c in range(NC):
             def body(i, carry, c=c):
                 rows = pl.ds(pl.multiple_of(i * 128, 128), 128)
-                source = pl.ds(pl.multiple_of(starts[c] + i * 128, 128), 128)
+                source = pl.ds(pl.multiple_of(start + c * PAIR + i * 128, 128), 128)
                 kg_v[k, rows, c * W:(c + 1) * W] = gg_v[source, :].astype(F32) * factor
                 return carry
 
             lax.fori_loop(0, C // 128, body, 0)
-        stores[k].start()
-
-    load[0].wait()
-    spread(1, [KG1_AT + c * C for c in range(NC)])
-    load[1].wait()
+        stores[3 + k].start()
+
+    spread(1, KG1_AT)
+    spread(0, KG02_AT)
+    spread(2, KG02_AT + C)
     for c in range(H // W):
         for j in range(C // W):
-            at = MG_AT + (c * (C // W) + j) * W
+            at = MG_AT + c * PAIR + j * W
             mg_v[c * W:(c + 1) * W, j * W:(j + 1) * W] = gg_v[at:at + W, :].astype(F32) * factor
-    stores[3].start()
-    load[2].wait()
-    spread(0, [KG02_AT + c * 2 * C for c in range(NC)])
-    spread(2, [KG02_AT + c * 2 * C + C for c in range(NC)])
-    for copy in copies + stores:
+    for copy in stores[2::-1]:
+        copy.start()
+    vec = vec_in[...] * factor
+    biases_out[...] = vec[:C // W].reshape(C)
+    offset_out[...] = vec[C // W:(C + H) // W].reshape(H)
+    for copy in stores:
         copy.wait()
 
 
 def local(features, kernel, offsets, mixer, biases, cotangent):
     length = features.shape[0] * lax.axis_size("seq") * lax.axis_size("sub")
     factor = 1.0 / math.sqrt(length)
-    any_spec = pl.BlockSpec(memory_space=pl.ANY)
+    hbm_spec = pl.BlockSpec(memory_space=pltpu.HBM)
     vmem_spec = pl.BlockSpec(memory_space=pltpu.VMEM)
     n = len(SEGS)
     vm = pltpu.VMEM
@@ -629,44 +699,47 @@
             jax.ShapeDtypeStruct((TOTAL, W), BF),
             jax.ShapeDtypeStruct((VEC, W), F32),
         ),
-        in_specs=[any_spec, any_spec, vmem_spec, any_spec, vmem_spec, any_spec],
-        out_specs=(any_spec, any_spec, any_spec, vmem_spec),
+        in_specs=[hbm_spec] * 6,
+        out_specs=(vmem_spec,) * 4,
         scratch_shapes=[
-            vm((ROWS, C), BF), vm((ROWS, C), BF), vm((NC, C, 2 * W), BF), vm((C, H), BF), vm((H, C), BF),
+            vm((ROWS, C), BF), vm((ROWS, C), BF), vm((NC, C, 2 * W), BF), vm((C, H), BF), vm((H, C), BF), vm((H,), F32), vm((C,), F32),
             vm((ROWS, C), BF), vm((C, ROWS), BF), vm((ROWS, C), F32), vm((ROWS, H), F32), vm((ROWS, H), F32),
             vm((NC, ROWS, W), BF), vm((NC, ROWS, W), BF), vm((NC, ROWS, W), BF), vm((NC, ROWS, W), BF),
             vm((ROWS, H), BF), vm((H, ROWS), BF), vm((ROWS, H), BF), vm((NC, ROWS, 2 * W), BF),
-            vm((ROWS, C), BF), vm((ROWS, C), BF), vm((TOTAL, W), F32),
+            vm((TOTAL, W), F32),
             vm((TOTAL // 2, W), BF), vm((TOTAL // 2, W), BF), vm((TOTAL // 2, W), BF), vm((TOTAL // 8 * 3, W), BF),
             vm((TOTAL // 8, W), BF), vm((TOTAL // 64 * 7, W), BF), vm((TOTAL // 64, W), BF),
-            vm((TOTAL // 64 * 4, W), BF), vm((TOTAL, W), BF),
+            vm((TOTAL // 64 * 4, W), BF),
+            vm((NP, SHARE, W), BF), vm((NP - 1, SHARE, W), BF), vm((NZ, SLICE, W), F32), vm((NZ, SLICE, W), BF),
+            vm((NZ - 1, SLICE, W), BF), vm((NZ, SLICE, W), BF),
             vm((4, VEC, W), F32), vm((2, VEC, W), F32), vm((NY, VEC, W), F32), vm((NZ, VEC, W), F32),
             vm((NX, VEC, W), F32),
-            dma((NR,)), dma((2 * NC + 3,)), dma((2 + n,)), dma((4,)), dma((2, NC, NR)), dma((2, NC, NR)),
+            dma((NR,)), dma((2 * NC + 5,)), dma((4,)), dma((2, NC, NR)), dma((2, NC, NR)),
             dma((n, 7)), dma((n, 7)), dma((4,)), dma((4,)),
         ],
         compiler_params=pltpu.CompilerParams(
-            collective_id=0, has_side_effects=True, vmem_limit_bytes=60 * 2**20
+            collective_id=0, has_side_effects=True, vmem_limit_bytes=46 * 2**20
         ),
         cost_estimate=pl.CostEstimate(flops=8_000_000_000, bytes_accessed=16_000_000, transcendentals=1_200_000),
         name="block",
-    )(features, kernel, offsets.reshape(1, H), mixer, biases.reshape(1, C), cotangent)
-    layer_output, input_grad, kernel_grad, mixer_grad = pl.pallas_call(
+    )(*[pltpu.with_memory_space_constraint(v, pltpu.HBM) for v in (features, kernel, offsets, mixer, biases, cotangent)])
+    layer_output, input_grad, kernel_grad, mixer_grad, offset_grad, biases_grad = pl.pallas_call(
         lambda *refs: finish_kernel(factor, *refs),
         out_shape=(
             jax.ShapeDtypeStruct((ROWS, C), BF),
             jax.ShapeDtypeStruct((ROWS, C), BF),
             jax.ShapeDtypeStruct((3, C, H), F32),
             jax.ShapeDtypeStruct((H, C), F32),
+            jax.ShapeDtypeStruct((H,), F32),
+            jax.ShapeDtypeStruct((C,), F32),
         ),
-        in_specs=[any_spec] * 3,
-        out_specs=(any_spec,) * 4,
-        scratch_shapes=[vm((TOTAL, W), BF), vm((3, C, H), F32), vm((H, C), F32), dma((9,))],
-        compiler_params=pltpu.CompilerParams(vmem_limit_bytes=24 * 2**20),
+        in_specs=[vmem_spec] * 4,
+        out_specs=(hbm_spec,) * 4 + (vmem_spec,) * 2,
+        scratch_shapes=[vm((3, C, H), F32), vm((H, C), F32), dma((6,))],
+        compiler_params=pltpu.CompilerParams(vmem_limit_bytes=12 * 2**20),
         name="finish",
-    )(lo, ig, gg)
-    sums = vec.reshape(VEC * W) * factor
-    return (layer_output, input_grad, kernel_grad, sums[C:C + H], mixer_grad, sums[:C])
+    )(lo, ig, gg, vec)
+    return (layer_output, input_grad, kernel_grad, offset_grad, mixer_grad, biases_grad)
 
 
 def solution(mesh):

time: 106 us -> 88.4 us (0.83)
  Pallas kernels: 96.7 us -> 87.7 us
  local copies, waits for them, and re-layouts: 8.17 us -> 0 us
    pallas_call x1, Pallas kernels: 93 us -> 83.7 us  [local(): pl.pallas_call(main_kernel, out_shape=(jax.ShapeDtypeStruct((ROWS, C), BF...]
    unnamed x6 -> x0, local copies, waits for them, and re-layouts: 4.48 us -> none
    reshape x2 -> x0, local copies, waits for them, and re-layouts: 2.51 us -> none  [the longest x1 1.27 us: local(): biases.reshape(1, C)]
    slice x2 -> x0, local copies, waits for them, and re-layouts: 1.18 us -> none  [the longest x1 0.59 us: local(): sums[:C]]
where the time goes in v3:
time: 88.4 us; the launch traced here: 88.3 us
  Pallas kernels  87.7 us (99%)
    pallas_call x1, Pallas kernels, local(): pl.pallas_call(main_kernel, out_shape=(jax.ShapeDtypeStruct((ROWS, C), BF...  83.7 us
    pallas_call x1, Pallas kernels, local(): pl.pallas_call(lambda *refs: finish_kernel(factor, *refs), out_shape=(jax...  3.98 us

profile of v3, /device:TPU:1, one launch (start us, length us, event | category | flops | bytes accessed | tf_op | source)
XLA Modules:
  0.0 88.3 jit_solution(1851499651339650135)
XLA Ops:
  0.6 83.7 %block.1 = (bf16[1024,768]{1,0:T(8,128)(2,1)S(1)}, bf16[1024,768]{1,0:T(8,128)(2,1)S(1)}, bf16[9216,128]{1,0:T(8,128)(2,1)S(1)}, f32[16,128]{1,0:T(8,128)S(1)}) custom-call(bf16[1024,768]{1,0:T(8,128)(2,1)} %f_hbm.1, bf16[3,768,384]{2,1,0:T(8,128)(2,1)} %k_hbm.1, f32[384]{0:T(512)} %off_hbm.1, bf16[384,768]{1,0:T(8,128)(2,1)} %mix_hbm.1, f32[768]{0:T(1024)} %bias_hbm.1, ...), custom_call_target="tpu_custom_call" | custom-call | flops 8000000000 | bytes 16000000 | tf_op jit(solution)/shard_map/block/pallas_call | solution.py:694
  84.3 4.0 %finish.1 = (bf16[1024,768]{1,0:T(8,128)(2,1)}, bf16[1024,768]{1,0:T(8,128)(2,1)}, f32[3,768,384]{2,1,0:T(8,128)}, f32[384,768]{1,0:T(8,128)}, f32[384]{0:T(512)}, /*index=5*/f32[768]{0:T(1024)}) custom-call(bf16[1024,768]{1,0:T(8,128)(2,1)S(1)} %get-tuple-element.16.refs_0_, bf16[1024,768]{1,0:T(8,128)(2,1)S(1)} %get-tuple-element.17.refs_1_, ...), custom_call_target="tpu_custom_call" | custom-call | tf_op jit(solution)/shard_map/finish/pallas_call | solution.py:726

commit v4 on v3

--- a/solution.py
+++ b/solution.py
@@ -25,11 +25,10 @@
 PAIR = 2 * C
 KG1_AT, MG_AT, KG02_AT = 0, C, NC * PAIR
 TOTAL = 2 * NC * PAIR
-SEGS = ((0, 3072), (3072, 3072), (6144, 1024), (7168, 2048))
-LAST = len(SEGS) - 1
+SEGS = ((0, 3072), (3072, 3072), (6144, 1536), (7680, 1536))
+LATE = 2
 NP = NX * NY
-SHARE = SEGS[LAST][1] // (2 * NP)
-SLICE = SHARE // NZ
+SHARE = SEGS[LATE][1] // (2 * NP)
 VEC = 16
 
 T_SCALE = 0.3
@@ -83,7 +82,7 @@
     act_v, actt_v, slope_v, pre_v, hg_v,
     t0_v, t2_v, te_v, tl_v, hid_v, hidt_v, pg_v, pg02_v,
     g_v, sbc, rbc, sby, rby, sbz, rbz, sbx, rbx,
-    last_s, last_r, last_own, last_zs, last_zr, last_g,
+    late_s, late_r, late_zs, late_z,
     vs, vc, vy, vz, vx,
     f_sem, in_sem, halo_send, tap_recv, pg_recv, seg_send, seg_recv, vec_send, vec_recv,
 ):
@@ -273,16 +272,19 @@
 
     CORE, Y, Z, X, GZ, GY, GC = range(7)
 
-    def place(s):
-        at, n = SEGS[s]
-        half, quarter, part = n // 2, n // 8, n // 64
-        own_half = at + core * half
-        own_quarter = own_half + y * quarter
-        own_part = own_quarter + z * part
-        return at, half, quarter, part, own_half, own_quarter, own_part
-
     def ds(base, n):
         return pl.ds(pl.multiple_of(base, 16), n)
+
+    def sizes(s):
+        at, n = SEGS[s]
+        return at, n // 2, n // 8, n // 64
+
+    def own_half(s):
+        at, half, *_ = sizes(s)
+        return at + core * half
+
+    def part_at(s, ty, tz):
+        return (ty * NZ + tz if s == 0 else tz * NY + ty) * sizes(s)[3]
 
     def send(s, stage, src, dst, to):
         pltpu.make_async_remote_copy(
@@ -290,28 +292,38 @@
             device_id=to, device_id_type=MESH,
         ).start()
 
-    def total(s, stage, ref):
-        return pltpu.make_async_remote_copy(
-            src_ref=ref, dst_ref=ref, send_sem=seg_send.at[s, stage], recv_sem=seg_recv.at[s, stage],
-            device_id=sibling, device_id_type=MESH,
-        )
+    def each(n, body):
+        def step(d, carry):
+            body(d)
+            return carry
+
+        lax.fori_loop(1, n, step, 0)
 
     def bulk(s, stage):
-        at, half, quarter, part, *_ = place(s)
-        if s == LAST and stage in (Y, GY):
-            return last_r
-        if s == LAST and stage in (Z, GZ):
-            return last_zr
+        at, half, quarter, part = sizes(s)
         if stage in (CORE, GC):
             return rbc.at[pl.ds(at // 2, half)]
+        if s >= LATE:
+            return late_z.at[s - LATE, pl.ds(0, NZ - 1)] if stage == Z else late_r.at[s - LATE]
+        if s == 1 and stage == GY:
+            return rbc.at[pl.ds(at // 2, (NY - 1) * part)]
+        if s == 1 and stage == GZ:
+            return rbc.at[pl.ds(at // 2, (NZ - 1) * NY * part)]
         if stage in (Y, GY):
             return rby.at[pl.ds(at // 8 * 3, 3 * quarter)]
         if stage in (Z, GZ):
             return rbz.at[pl.ds(at // 64 * 7, 7 * part)]
         return rbx.at[pl.ds(at // 64 * 4, 3 * part)]
 
+    def total(s, stage):
+        ref = bulk(s, stage)
+        return pltpu.make_async_remote_copy(
+            src_ref=ref, dst_ref=ref, send_sem=seg_send.at[s, stage], recv_sem=seg_recv.at[s, stage],
+            device_id=sibling, device_id_type=MESH,
+        )
+
     def core_send(s):
-        at, half, *_ = place(s)
+        at, half, *_ = sizes(s)
         other = at + (1 - core) * half
 
         def body(i):
@@ -324,164 +336,133 @@
         send(s, CORE, sbc.at[rows], rbc.at[rows], sibling)
 
     def y_send(s):
-        at, half, quarter, part, own_half, own_quarter, own_part = place(s)
-        total(s, CORE, bulk(s, CORE)).wait_recv()
+        at, half, quarter, part = sizes(s)
+        total(s, CORE).wait_recv()
 
         def body(i):
-            rows = ds(own_half + i * 128, 128)
+            rows = ds(own_half(s) + i * 128, 128)
             got = pl.ds(pl.multiple_of(at // 2 + i * 128, 128), 128)
             summed = g_v[rows, :] + rbc[got, :].astype(F32)
             g_v[rows, :] = summed
             sby[got, :] = summed.astype(BF)
 
         loop(half // 128, body)
-
-        def to(d, carry):
-            ty = lax.rem(y + d, NY)
-            send(
-                s, Y, sby.at[ds(at // 2 + ty * quarter, quarter)],
+        if s == 0:
+            each(NY, lambda d: send(
+                s, Y, sby.at[ds(at // 2 + part_at(s, lax.rem(y + d, NY), 0), quarter)],
                 rby.at[ds(at // 8 * 3 + (d - 1) * quarter, quarter)], y_peer(d),
-            )
-            return carry
-
-        lax.fori_loop(1, NY, to, 0)
+            ))
+        else:
+            def blocks(i):
+                d, tz = 1 + lax.div(i, NZ), lax.rem(i, NZ)
+                send(
+                    s, Y, sby.at[ds(at // 2 + part_at(s, lax.rem(y + d, NY), tz), part)],
+                    rby.at[ds(at // 8 * 3 + (d - 1) * quarter + tz * part, part)], y_peer(d),
+                )
+
+            loop((NY - 1) * NZ, blocks)
 
     def z_send(s):
-        at, half, quarter, part, own_half, own_quarter, own_part = place(s)
-        total(s, Y, bulk(s, Y)).wait_recv()
+        at, half, quarter, part = sizes(s)
+        total(s, Y).wait_recv()
 
         def body(i):
-            rows = ds(own_quarter + i * 64, 64)
+            rows = ds(own_half(s) + part_at(s, y, i), part)
             summed = g_v[rows, :]
             for d in range(NY - 1):
-                summed = summed + rby[ds(at // 8 * 3 + d * quarter + i * 64, 64), :].astype(F32)
+                summed = summed + rby[ds(at // 8 * 3 + d * quarter + i * part, part), :].astype(F32)
             g_v[rows, :] = summed
-            sbz[ds(at // 8 + i * 64, 64), :] = summed.astype(BF)
-
-        loop(quarter // 64, body)
-
-        def to(d, carry):
-            tz = lax.rem(z + d, NZ)
-            send(
-                s, Z, sbz.at[ds(at // 8 + tz * part, part)],
-                rbz.at[ds(at // 64 * 7 + (d - 1) * part, part)], z_peer(d),
-            )
-            return carry
-
-        lax.fori_loop(1, NZ, to, 0)
+            sbz[ds(at // 8 + i * part, part), :] = summed.astype(BF)
+
+        loop(NZ, body)
+        each(NZ, lambda d: send(
+            s, Z, sbz.at[ds(at // 8 + lax.rem(z + d, NZ) * part, part)],
+            rbz.at[ds(at // 64 * 7 + (d - 1) * part, part)], z_peer(d),
+        ))
 
     def x_send(s):
-        at, half, quarter, part, own_half, own_quarter, own_part = place(s)
-        total(s, Z, bulk(s, Z)).wait_recv()
-        summed = g_v[ds(own_part, part), :]
+        at, half, quarter, part = sizes(s)
+        total(s, Z).wait_recv()
+        summed = g_v[ds(own_half(s) + part_at(s, y, z), part), :]
         for d in range(NZ - 1):
             summed = summed + rbz[ds(at // 64 * 7 + d * part, part), :].astype(F32)
-        mine = rbx.at[ds(at // 64 * 4 + x * part, part)]
+        rows = ds(at // 64 * 4 + x * part, part)
         sbx[pl.ds(at // 64, part), :] = summed.astype(BF)
-        rbx[ds(at // 64 * 4 + x * part, part), :] = summed.astype(BF)
-
-        def to(d, carry):
-            send(s, X, sbx.at[pl.ds(at // 64, part)], mine, x_peer(d))
-            return carry
-
-        lax.fori_loop(1, NX, to, 0)
-
-    def z_gather(s):
-        at, half, quarter, part, own_half, own_quarter, own_part = place(s)
-        total(s, X, bulk(s, X)).wait_recv()
+        rbx[rows, :] = summed.astype(BF)
+        each(NX, lambda d: send(s, X, sbx.at[pl.ds(at // 64, part)], rbx.at[rows], x_peer(d)))
+
+    def summed_over_x(s):
+        at, half, quarter, part = sizes(s)
+        total(s, X).wait_recv()
         summed = rbx[pl.ds(at // 64 * 4, part), :].astype(F32)
         for k in range(1, NX):
             summed = summed + rbx[pl.ds(at // 64 * 4 + k * part, part), :].astype(F32)
-        gg_v[ds(own_part, part), :] = summed.astype(BF)
-        ref = gg_v.at[ds(own_part, part)]
-
-        def to(d, carry):
-            send(s, GZ, ref, ref, z_peer(d))
-            return carry
-
-        lax.fori_loop(1, NZ, to, 0)
-
-    def y_gather(s):
-        at, half, quarter, part, own_half, own_quarter, own_part = place(s)
-        total(s, GZ, bulk(s, GZ)).wait_recv()
-        ref = gg_v.at[ds(own_quarter, quarter)]
-
-        def to(d, carry):
-            send(s, GY, ref, ref, y_peer(d))
-            return carry
-
-        lax.fori_loop(1, NY, to, 0)
+        rows = ds(own_half(s) + part_at(s, y, z), part)
+        gg_v[rows, :] = summed.astype(BF)
+        return gg_v.at[rows]
+
+    def gather(s):
+        ref = summed_over_x(s)
+        if s == 0:
+            each(NZ, lambda d: send(s, GZ, ref, ref, z_peer(d)))
+        else:
+            each(NY, lambda d: send(s, GY, ref, ref, y_peer(d)))
+
+    def gather_more(s):
+        at, half, quarter, part = sizes(s)
+        if s == 0:
+            total(s, GZ).wait_recv()
+            ref = gg_v.at[ds(own_half(s) + part_at(s, y, 0), quarter)]
+            each(NY, lambda d: send(s, GY, ref, ref, y_peer(d)))
+        else:
+            total(s, GY).wait_recv()
+            ref = gg_v.at[ds(own_half(s) + part_at(s, 0, z), NY * part)]
+            each(NZ, lambda d: send(s, GZ, ref, ref, z_peer(d)))
+
+    def late_rows(s):
+        return ds(own_half(s) + xy_at(0) * SHARE, SHARE)
+
+    def xy_send(s):
+        at, half, *_ = sizes(s)
+        k = s - LATE
+        total(s, CORE).wait_recv()
+
+        def body(i):
+            rows = ds(own_half(s) + i * SHARE, SHARE)
+            summed = g_v[rows, :] + rbc[ds(at // 2 + i * SHARE, SHARE), :].astype(F32)
+            g_v[rows, :] = summed
+            late_s[k, i] = summed.astype(BF)
+
+        loop(NP, body)
+        each(NP, lambda d: send(s, Y, late_s.at[k, xy_at(d)], late_r.at[k, d - 1], xy_peer(d)))
+
+    def z_all(s):
+        k = s - LATE
+        total(s, Y).wait_recv()
+        summed = g_v[late_rows(s), :]
+        for d in range(NP - 1):
+            summed = summed + late_r[k, d].astype(F32)
+        late_zs[k] = summed.astype(BF)
+        late_z[k, z] = summed.astype(BF)
+        each(NZ, lambda d: send(s, Z, late_zs.at[k], late_z.at[k, z], z_peer(d)))
+
+    def xy_gather(s):
+        k = s - LATE
+        total(s, Z).wait_recv()
+        summed = late_z[k, 0].astype(F32)
+        for i in range(1, NZ):
+            summed = summed + late_z[k, i].astype(F32)
+        gg_v[late_rows(s), :] = summed.astype(BF)
+        ref = gg_v.at[late_rows(s)]
+        each(NP, lambda d: send(s, GY, ref, ref, xy_peer(d)))
 
     def core_gather(s):
-        at, half, quarter, part, own_half, own_quarter, own_part = place(s)
-        total(s, GY, bulk(s, GY)).wait_recv()
-        ref = gg_v.at[ds(own_half, half)]
+        total(s, GZ if s == 1 else GY).wait_recv()
+        ref = gg_v.at[ds(own_half(s), sizes(s)[1])]
         send(s, GC, ref, ref, sibling)
 
-    last_half = SEGS[LAST][0] + core * (SEGS[LAST][1] // 2)
-
-    def last_xy():
-        at, half, *_ = place(LAST)
-        total(LAST, CORE, bulk(LAST, CORE)).wait_recv()
-
-        def body(i):
-            rows = ds(last_half + i * SHARE, SHARE)
-            got = pl.ds(pl.multiple_of(at // 2 + i * SHARE, SHARE), SHARE)
-            summed = g_v[rows, :] + rbc[got, :].astype(F32)
-            g_v[rows, :] = summed
-            last_s[i] = summed.astype(BF)
-
-        loop(NP, body)
-
-        def to(d, carry):
-            send(LAST, Y, last_s.at[xy_at(d)], last_r.at[d - 1], xy_peer(d))
-            return carry
-
-        lax.fori_loop(1, NP, to, 0)
-
-    def last_z():
-        total(LAST, Y, last_r).wait_recv()
-        summed = g_v[ds(last_half + xy_at(0) * SHARE, SHARE), :]
-        for d in range(NP - 1):
-            summed = summed + last_r[d].astype(F32)
-        summed = summed.reshape(NZ, SLICE, W)
-        last_own[...] = summed
-        last_zs[...] = summed.astype(BF)
-
-        def to(d, carry):
-            send(LAST, Z, last_zs.at[lax.rem(z + d, NZ)], last_zr.at[d - 1], z_peer(d))
-            return carry
-
-        lax.fori_loop(1, NZ, to, 0)
-
-    def last_z_gather():
-        total(LAST, Z, last_zr).wait_recv()
-        summed = last_own[z]
-        for d in range(NZ - 1):
-            summed = summed + last_zr[d].astype(F32)
-        last_g[z] = summed.astype(BF)
-        ref = last_g.at[z]
-
-        def to(d, carry):
-            send(LAST, GZ, ref, ref, z_peer(d))
-            return carry
-
-        lax.fori_loop(1, NZ, to, 0)
-
-    def last_xy_gather():
-        total(LAST, GZ, last_zr).wait_recv()
-        rows = ds(last_half + xy_at(0) * SHARE, SHARE)
-        gg_v[rows, :] = last_g[...].astype(F32).reshape(SHARE, W).astype(BF)
-        ref = gg_v.at[rows]
-
-        def to(d, carry):
-            send(LAST, GY, ref, ref, xy_peer(d))
-            return carry
-
-        lax.fori_loop(1, NP, to, 0)
-
     def finish(s):
-        total(s, GC, bulk(s, GC)).wait_recv()
+        total(s, GC).wait_recv()
 
     vec_stages = ((vc, 2, core, lambda d: sibling), (vy, NY, y, y_peer), (vz, NZ, z, z_peer), (vx, NX, x, x_peer))
 
@@ -592,44 +573,40 @@
     kg1_and_mixer(2, 1)
     vectors()
     vec_step(0)
-    loop(2, leave)
+    loop(NR, leave)
     z_send(0)
-    loop(2, lambda i: leave(i + 2))
+    vec_step(1)
     kg02(0)
     core_send(1)
-    vec_step(1)
+    vec_step(2)
     y_send(1)
-    x_send(0)
     kg02(1)
     core_send(2)
-    z_gather(0)
-    y_send(2)
-    vec_step(2)
+    kg02(2)
+    core_send(3)
+    xy_send(2)
     z_send(1)
-    kg02(2)
-    core_send(LAST)
-    z_send(2)
-    y_gather(0)
-    last_xy()
+    xy_send(3)
+    grad_in(0)
+    x_send(0)
+    grad_in(1)
+    vec_step(3)
+    z_all(2)
+    gather(0)
     x_send(1)
-    x_send(2)
-    z_gather(1)
-    grad_in(0)
+    z_all(3)
+    grad_in(2)
+    gather(1)
+    gather_more(0)
+    xy_gather(2)
+    gather_more(1)
+    xy_gather(3)
+    grad_in(3)
+    vec_step(4)
     core_gather(0)
-    z_gather(2)
-    last_z()
-    vec_step(3)
-    grad_in(1)
-    y_gather(1)
-    last_z_gather()
-    y_gather(2)
-    grad_in(2)
-    last_xy_gather()
-    grad_in(3)
+    core_gather(2)
     core_gather(1)
-    core_gather(2)
-    vec_step(4)
-    core_gather(LAST)
+    core_gather(3)
     for s in range(len(SEGS)):
         finish(s)
 
@@ -642,8 +619,8 @@
         vec_all(stage).wait_send()
     for s in range(len(SEGS)):
         for stage in range(7):
-            if s != LAST or stage != X:
-                total(s, stage, bulk(s, stage)).wait_send()
+            if s < LATE or stage not in (X, GZ):
+                total(s, stage).wait_send()
 
 
 def finish_kernel(
@@ -710,8 +687,7 @@
             vm((TOTAL // 2, W), BF), vm((TOTAL // 2, W), BF), vm((TOTAL // 2, W), BF), vm((TOTAL // 8 * 3, W), BF),
             vm((TOTAL // 8, W), BF), vm((TOTAL // 64 * 7, W), BF), vm((TOTAL // 64, W), BF),
             vm((TOTAL // 64 * 4, W), BF),
-            vm((NP, SHARE, W), BF), vm((NP - 1, SHARE, W), BF), vm((NZ, SLICE, W), F32), vm((NZ, SLICE, W), BF),
-            vm((NZ - 1, SLICE, W), BF), vm((NZ, SLICE, W), BF),
+            vm((2, NP, SHARE, W), BF), vm((2, NP - 1, SHARE, W), BF), vm((2, SHARE, W), BF), vm((2, NZ, SHARE, W), BF),
             vm((4, VEC, W), F32), vm((2, VEC, W), F32), vm((NY, VEC, W), F32), vm((NZ, VEC, W), F32),
             vm((NX, VEC, W), F32),
             dma((NR,)), dma((2 * NC + 5,)), dma((4,)), dma((2, NC, NR)), dma((2, NC, NR)),

time: 88.4 us -> 82.1 us (0.929)
  Pallas kernels: 87.7 us -> 81.4 us
    pallas_call x1, Pallas kernels: 83.7 us -> 77.4 us  [local(): pl.pallas_call(main_kernel, out_shape=(jax.ShapeDtypeStruct((ROWS, C), BF...]
where the time goes in v4:
time: 82.1 us; the launch traced here: 82 us
  Pallas kernels  81.4 us (99%)
    pallas_call x1, Pallas kernels, local(): pl.pallas_call(main_kernel, out_shape=(jax.ShapeDtypeStruct((ROWS, C), BF...  77.4 us
    pallas_call x1, Pallas kernels, local(): pl.pallas_call(lambda *refs: finish_kernel(factor, *refs), out_shape=(jax...  3.98 us

profile of v4, /device:TPU:1, one launch (start us, length us, event | category | flops | bytes accessed | tf_op | source)
XLA Modules:
  0.0 82.0 jit_solution(4918118218891978239)
XLA Ops:
  0.6 77.4 %block.1 = (bf16[1024,768]{1,0:T(8,128)(2,1)S(1)}, bf16[1024,768]{1,0:T(8,128)(2,1)S(1)}, bf16[9216,128]{1,0:T(8,128)(2,1)S(1)}, f32[16,128]{1,0:T(8,128)S(1)}) custom-call(bf16[1024,768]{1,0:T(8,128)(2,1)} %f_hbm.1, bf16[3,768,384]{2,1,0:T(8,128)(2,1)} %k_hbm.1, f32[384]{0:T(512)} %off_hbm.1, bf16[384,768]{1,0:T(8,128)(2,1)} %mix_hbm.1, f32[768]{0:T(1024)} %bias_hbm.1, ...), custom_call_target="tpu_custom_call" | custom-call | flops 8000000000 | bytes 16000000 | tf_op jit(solution)/shard_map/block/pallas_call | solution.py:671
  78.0 4.0 %finish.1 = (bf16[1024,768]{1,0:T(8,128)(2,1)}, bf16[1024,768]{1,0:T(8,128)(2,1)}, f32[3,768,384]{2,1,0:T(8,128)}, f32[384,768]{1,0:T(8,128)}, f32[384]{0:T(512)}, /*index=5*/f32[768]{0:T(1024)}) custom-call(bf16[1024,768]{1,0:T(8,128)(2,1)S(1)} %get-tuple-element.16.refs_0_, bf16[1024,768]{1,0:T(8,128)(2,1)S(1)} %get-tuple-element.17.refs_1_, ...), custom_call_target="tpu_custom_call" | custom-call | tf_op jit(solution)/shard_map/finish/pallas_call | solution.py:702

commit v5 on v4

--- a/solution.py
+++ b/solution.py
@@ -19,6 +19,7 @@
 NC = H // W
 NR = 4
 RB = ROWS // NR
+NB = ROWS // 256
 
 NX, NY, NZ = 4, 4, 8
 
@@ -79,7 +80,7 @@
     f_hbm, k_hbm, off_hbm, mix_hbm, bias_hbm, cot_hbm,
     lo_v, ig_v, gg_v, vec_ref,
     f_v, cot_v, kw_v, k1_v, mix_v, off_v, bias_v,
-    act_v, actt_v, slope_v, pre_v, hg_v,
+    act_v, actt_v, slope_v, grad_v, pre_v, hg_v,
     t0_v, t2_v, te_v, tl_v, hid_v, hidt_v, pg_v, pg02_v,
     g_v, sbc, rbc, sby, rby, sbz, rbz, sbx, rbx,
     late_s, late_r, late_zs, late_z,
@@ -138,9 +139,13 @@
     f_copy(0).start()
     ins[0].start()
     ins[1].start()
-    for r in range(1, NR):
+    for r in range(1, 3):
         f_copy(r).start()
-    for copy in ins[2:]:
+    ins[2].start()
+    ins[3].start()
+    for r in range(3, NR):
+        f_copy(r).start()
+    for copy in ins[4:]:
         copy.start()
 
     greet(sibling)
@@ -193,46 +198,47 @@
         for copy in tap_copies(c, r):
             copy.start()
 
-    with jax.named_scope("start"):
-        f_copy(0).wait()
-        activate(0)
-        ins[0].wait()
-        ins[1].wait()
-        taps(0, 0)
-    with jax.named_scope("greeted"):
-        pl.semaphore_wait(barrier, 1 + 2 + (NP - 1) + (NZ - 1))
+    def taps_of_two(r):
+        for c in range(2):
+            taps(c, r)
+        for c in range(2):
+            send_taps(c, r)
+
+    f_copy(0).wait()
+    activate(0)
+    for copy in ins[:4]:
+        copy.wait()
+    taps(0, 0)
+    pl.semaphore_wait(barrier, 1 + 2 + (NP - 1) + (NZ - 1))
     send_taps(0, 0)
+    taps(1, 0)
+    send_taps(1, 0)
 
     def first(i):
         r = i + 1
         f_copy(r).wait()
         activate(r)
-        taps(0, r)
-        send_taps(0, r)
-
-    with jax.named_scope("first"):
-        loop(NR - 1, first)
-    for c in range(1, NC):
-        ins[2 * c].wait()
-        ins[2 * c + 1].wait()
-
-        def more(r, c=c):
-            taps(c, r)
-            send_taps(c, r)
-
-        with jax.named_scope("more_taps"):
-            loop(NR, more)
-
+        taps_of_two(r)
+
+    loop(NR - 1, first)
+    for copy in ins[4:6]:
+        copy.wait()
+
+    def third(r):
+        taps(2, r)
+        send_taps(2, r)
+
+    loop(NR, third)
     for copy in ins[2 * NC:]:
         copy.wait()
 
     def own(r):
-        rows = pl.ds(pl.multiple_of(r * RB, RB), RB)
+        rows = pl.ds(pl.multiple_of(r * 256, 256), 256)
         pre_v[rows, :] = nn(act_v[rows, :], k1_v[...]) + off_v[...].reshape(1, H)
         hg_v[rows, :] = nt(cot_v[rows, :], mix_v[...])
 
     with jax.named_scope("own"):
-        loop(NR, own)
+        loop(NB, own)
 
     def pg_copies(c, r):
         rows = pl.ds(pl.multiple_of(r * RB, RB), RB)
@@ -331,7 +337,8 @@
                 ds(other + i * 128, 128), :
             ].astype(BF)
 
-        loop(half // 128, body)
+        if s < LATE:
+            loop(half // 128, body)
         rows = pl.ds(at // 2, half)
         send(s, CORE, sbc.at[rows], rbc.at[rows], sibling)
 
@@ -501,14 +508,14 @@
         lax.fori_loop(1, n, to, 0)
 
     def transpose(r):
-        for r in range(NR):
-            rows = pl.ds(r * RB, RB)
+        for r in range(NB):
+            rows = pl.ds(r * 256, 256)
             actt_v[:, rows] = act_v[rows, :].T
 
     def kg1_and_mixer(c, n):
         lanes = slice(c * W, (c + n) * W)
-        for r in range(NR):
-            rows = pl.ds(r * RB, RB)
+        for r in range(NB):
+            rows = pl.ds(r * 256, 256)
             hidt_v[lanes, rows] = hid_v[rows, lanes].T
 
         def kg1(m):
@@ -545,20 +552,32 @@
 
         def block(m):
             part = nn(actt_v[pl.ds(pl.multiple_of(m * 256, 256), 256), :], pg02_v[c])
-            at = KG02_AT + c * PAIR + m * 256
-            g_v[pl.ds(pl.multiple_of(at, 256), 256), :] = part[:, :W]
-            g_v[pl.ds(pl.multiple_of(at + C, 256), 256), :] = part[:, W:]
+            early, late = part[:, :W], part[:, W:]
+            if c == 0:
+                at = KG02_AT + m * 256
+                g_v[pl.ds(pl.multiple_of(at, 256), 256), :] = early
+                g_v[pl.ds(pl.multiple_of(at + C, 256), 256), :] = late
+            else:
+                s = LATE + c - 1
+                g_v[pl.ds(pl.multiple_of(own_half(s) + m * 256, 256), 256), :] = jnp.where(core == 0, early, late)
+                sbc[pl.ds(pl.multiple_of(SEGS[s][0] // 2 + m * 256, 256), 256), :] = jnp.where(
+                    core == 0, late, early
+                ).astype(BF)
 
         loop(C // 256, block)
 
     def leave(r):
-        rows = pl.ds(pl.multiple_of(r * RB, RB), RB)
+        rows = pl.ds(pl.multiple_of(r * 256, 256), 256)
         lo_v[rows, :] = (f_v[rows, :].astype(F32) + nn(hid_v[rows, :], mix_v[...]) + bias_v[...].reshape(1, C)).astype(BF)
 
+    def grad_part(r):
+        rows = pl.ds(pl.multiple_of(r * 256, 256), 256)
+        grad_v[rows, :] = nt(pg_v[rows, :], k1_v[...]) + nt(pg02_v[0, rows, :], kw_v[0])
+
     def grad_in(r):
-        rows = pl.ds(pl.multiple_of(r * RB, RB), RB)
-        grad = nt(pg_v[rows, :], k1_v[...])
-        for c in range(NC):
+        rows = pl.ds(pl.multiple_of(r * 256, 256), 256)
+        grad = grad_v[rows, :]
+        for c in range(1, NC):
             grad = grad + nt(pg02_v[c, rows, :], kw_v[c])
         ig_v[rows, :] = (cot_v[rows, :].astype(F32) + grad * slope_v[rows, :]).astype(BF)
 
@@ -567,44 +586,45 @@
     hidden(1)
     kg1_and_mixer(0, 2)
     core_send(0)
-    hidden(2, 0, 2)
+    hidden(2, 0, NR // 2)
     y_send(0)
-    hidden(2, 2, NR)
+    hidden(2, NR // 2, NR)
     kg1_and_mixer(2, 1)
     vectors()
     vec_step(0)
-    loop(NR, leave)
+    loop(NB, leave)
     z_send(0)
     vec_step(1)
     kg02(0)
     core_send(1)
     vec_step(2)
     y_send(1)
+    loop(NB, grad_part)
     kg02(1)
     core_send(2)
+    z_send(1)
+    xy_send(2)
     kg02(2)
     core_send(3)
-    xy_send(2)
-    z_send(1)
+    x_send(0)
     xy_send(3)
+    x_send(1)
+    vec_step(3)
+    gather(0)
+    z_all(2)
+    gather(1)
+    z_all(3)
     grad_in(0)
-    x_send(0)
+    gather_more(1)
+    gather_more(0)
     grad_in(1)
-    vec_step(3)
-    z_all(2)
-    gather(0)
-    x_send(1)
-    z_all(3)
+    xy_gather(2)
+    xy_gather(3)
     grad_in(2)
-    gather(1)
-    gather_more(0)
-    xy_gather(2)
-    gather_more(1)
-    xy_gather(3)
     grad_in(3)
     vec_step(4)
+    core_gather(2)
     core_gather(0)
-    core_gather(2)
     core_gather(1)
     core_gather(3)
     for s in range(len(SEGS)):
@@ -633,6 +653,9 @@
     ]
     stores += [pltpu.make_async_copy(kg_v.at[k], kg_out.at[k], sem.at[3 + k]) for k in range(3)]
 
+    for copy in stores[:2]:
+        copy.start()
+
     def spread(k, start):
         for c in range(NC):
             def body(i, carry, c=c):
@@ -651,8 +674,7 @@
         for j in range(C // W):
             at = MG_AT + c * PAIR + j * W
             mg_v[c * W:(c + 1) * W, j * W:(j + 1) * W] = gg_v[at:at + W, :].astype(F32) * factor
-    for copy in stores[2::-1]:
-        copy.start()
+    stores[2].start()
     vec = vec_in[...] * factor
     biases_out[...] = vec[:C // W].reshape(C)
     offset_out[...] = vec[C // W:(C + H) // W].reshape(H)
@@ -680,7 +702,7 @@
         out_specs=(vmem_spec,) * 4,
         scratch_shapes=[
             vm((ROWS, C), BF), vm((ROWS, C), BF), vm((NC, C, 2 * W), BF), vm((C, H), BF), vm((H, C), BF), vm((H,), F32), vm((C,), F32),
-            vm((ROWS, C), BF), vm((C, ROWS), BF), vm((ROWS, C), F32), vm((ROWS, H), F32), vm((ROWS, H), F32),
+            vm((ROWS, C), BF), vm((C, ROWS), BF), vm((ROWS, C), F32), vm((ROWS, C), F32), vm((ROWS, H), F32), vm((ROWS, H), F32),
             vm((NC, ROWS, W), BF), vm((NC, ROWS, W), BF), vm((NC, ROWS, W), BF), vm((NC, ROWS, W), BF),
             vm((ROWS, H), BF), vm((H, ROWS), BF), vm((ROWS, H), BF), vm((NC, ROWS, 2 * W), BF),
             vm((TOTAL, W), F32),

time: 82.1 us -> 78.2 us (0.952)
  Pallas kernels: 81.4 us -> 77.5 us
    pallas_call x1, Pallas kernels: 77.4 us -> 73.7 us  [local(): pl.pallas_call(main_kernel, out_shape=(jax.ShapeDtypeStruct((ROWS, C), BF...]
where the time goes in v5:
time: 78.2 us; the launch traced here: 78.1 us
  Pallas kernels  77.5 us (99%)
    pallas_call x1, Pallas kernels, local(): pl.pallas_call(main_kernel, out_shape=(jax.ShapeDtypeStruct((ROWS, C), BF...  73.7 us
    pallas_call x1, Pallas kernels, local(): pl.pallas_call(lambda *refs: finish_kernel(factor, *refs), out_shape=(jax...  3.79 us

profile of v5, /device:TPU:1, one launch (start us, length us, event | category | flops | bytes accessed | tf_op | source)
XLA Modules:
  0.0 78.1 jit_solution(13970817671003535237)
XLA Ops:
  0.6 73.7 %block.1 = (bf16[1024,768]{1,0:T(8,128)(2,1)S(1)}, bf16[1024,768]{1,0:T(8,128)(2,1)S(1)}, bf16[9216,128]{1,0:T(8,128)(2,1)S(1)}, f32[16,128]{1,0:T(8,128)S(1)}) custom-call(bf16[1024,768]{1,0:T(8,128)(2,1)} %f_hbm.1, bf16[3,768,384]{2,1,0:T(8,128)(2,1)} %k_hbm.1, f32[384]{0:T(512)} %off_hbm.1, bf16[384,768]{1,0:T(8,128)(2,1)} %mix_hbm.1, f32[768]{0:T(1024)} %bias_hbm.1, ...), custom_call_target="tpu_custom_call" | custom-call | flops 8000000000 | bytes 16000000 | tf_op jit(solution)/shard_map/block/pallas_call | solution.py:693
  74.3 3.8 %finish.1 = (bf16[1024,768]{1,0:T(8,128)(2,1)}, bf16[1024,768]{1,0:T(8,128)(2,1)}, f32[3,768,384]{2,1,0:T(8,128)}, f32[384,768]{1,0:T(8,128)}, f32[384]{0:T(512)}, /*index=5*/f32[768]{0:T(1024)}) custom-call(bf16[1024,768]{1,0:T(8,128)(2,1)S(1)} %get-tuple-element.16.refs_0_, bf16[1024,768]{1,0:T(8,128)(2,1)S(1)} %get-tuple-element.17.refs_1_, ...), custom_call_target="tpu_custom_call" | custom-call | tf_op jit(solution)/shard_map/finish/pallas_call | solution.py:724

commit v6 on v5

--- a/solution.py
+++ b/solution.py
@@ -651,21 +651,30 @@
         pltpu.make_async_copy(ig_v, ig_out, sem.at[1]),
         pltpu.make_async_copy(mg_v, mg_out, sem.at[2]),
     ]
-    stores += [pltpu.make_async_copy(kg_v.at[k], kg_out.at[k], sem.at[3 + k]) for k in range(3)]
+    stores += [
+        pltpu.make_async_copy(
+            kg_v.at[k, pl.ds(part * (C // 2), C // 2)], kg_out.at[k, pl.ds(part * (C // 2), C // 2)],
+            sem.at[3 + 2 * k + part],
+        )
+        for k in range(3)
+        for part in range(2)
+    ]
 
     for copy in stores[:2]:
         copy.start()
 
     def spread(k, start):
-        for c in range(NC):
-            def body(i, carry, c=c):
-                rows = pl.ds(pl.multiple_of(i * 128, 128), 128)
-                source = pl.ds(pl.multiple_of(start + c * PAIR + i * 128, 128), 128)
-                kg_v[k, rows, c * W:(c + 1) * W] = gg_v[source, :].astype(F32) * factor
-                return carry
-
-            lax.fori_loop(0, C // 128, body, 0)
-        stores[3 + k].start()
+        for part in range(2):
+            for c in range(NC):
+                def body(i, carry, c=c):
+                    at = (part * (C // 256) + i) * 128
+                    rows = pl.ds(pl.multiple_of(at, 128), 128)
+                    source = pl.ds(pl.multiple_of(start + c * PAIR + at, 128), 128)
+                    kg_v[k, rows, c * W:(c + 1) * W] = gg_v[source, :].astype(F32) * factor
+                    return carry
+
+                lax.fori_loop(0, C // 256, body, 0)
+            stores[3 + 2 * k + part].start()
 
     spread(1, KG1_AT)
     spread(0, KG02_AT)
@@ -733,7 +742,7 @@
         ),
         in_specs=[vmem_spec] * 4,
         out_specs=(hbm_spec,) * 4 + (vmem_spec,) * 2,
-        scratch_shapes=[vm((3, C, H), F32), vm((H, C), F32), dma((6,))],
+        scratch_shapes=[vm((3, C, H), F32), vm((H, C), F32), dma((9,))],
         compiler_params=pltpu.CompilerParams(vmem_limit_bytes=12 * 2**20),
         name="finish",
     )(lo, ig, gg, vec)

time: 78.2 us -> 78.2 us (level)
  no operation moved by 1% of the time
where the time goes in v6:
time: 78.2 us
  Pallas kernels  77.5 us (99%)
    pallas_call x1, Pallas kernels, local(): pl.pallas_call(main_kernel, out_shape=(jax.ShapeDtypeStruct((ROWS, C), BF...  73.7 us
    pallas_call x1, Pallas kernels, local(): pl.pallas_call(lambda *refs: finish_kernel(factor, *refs), out_shape=(jax...  3.82 us

profile of v6, /device:TPU:1, one launch (start us, length us, event | category | flops | bytes accessed | tf_op | source)
XLA Modules:
  0.0 78.2 jit_solution(17303430061500676441)
XLA Ops:
  0.6 73.7 %block.1 = (bf16[1024,768]{1,0:T(8,128)(2,1)S(1)}, bf16[1024,768]{1,0:T(8,128)(2,1)S(1)}, bf16[9216,128]{1,0:T(8,128)(2,1)S(1)}, f32[16,128]{1,0:T(8,128)S(1)}) custom-call(bf16[1024,768]{1,0:T(8,128)(2,1)} %f_hbm.1, bf16[3,768,384]{2,1,0:T(8,128)(2,1)} %k_hbm.1, f32[384]{0:T(512)} %off_hbm.1, bf16[384,768]{1,0:T(8,128)(2,1)} %mix_hbm.1, f32[768]{0:T(1024)} %bias_hbm.1, ...), custom_call_target="tpu_custom_call" | custom-call | flops 8000000000 | bytes 16000000 | tf_op jit(solution)/shard_map/block/pallas_call | solution.py:702
  74.3 3.8 %finish.1 = (bf16[1024,768]{1,0:T(8,128)(2,1)}, bf16[1024,768]{1,0:T(8,128)(2,1)}, f32[3,768,384]{2,1,0:T(8,128)}, f32[384,768]{1,0:T(8,128)}, f32[384]{0:T(512)}, /*index=5*/f32[768]{0:T(1024)}) custom-call(bf16[1024,768]{1,0:T(8,128)(2,1)S(1)} %get-tuple-element.16.refs_0_, bf16[1024,768]{1,0:T(8,128)(2,1)S(1)} %get-tuple-element.17.refs_1_, ...), custom_call_target="tpu_custom_call" | custom-call | tf_op jit(solution)/shard_map/finish/pallas_call | solution.py:733
